TPU v7x, 256 devices: a whole 4x4x8 slice. The times are simulated.
256 devices in a mesh: tm: 64 (over z, y, x_hi), chan: 4 (over x_lo, core).
Axes of the slice: x: 4 (x_hi: 2, x_lo: 2; x = x_hi * 2 + x_lo), y: 4, z: 8, core: 2. Of those that a mesh axis runs over, the one named last changes fastest.
Arguments:
- signal: bfloat16 [384, 8192], P('chan', 'tm'), may hold values from -6 to 6
- codes_init: float32 [128, 8192], P(None, 'tm'), may hold values from -2 to 2
- dictionary_init: float32 [128, 36864], P(None, 'chan'), may hold values from -6 to 6
- threshold: float32 [128], replicated, may hold values from 0.05 to 0.5
- plan: int32 [8], replicated, may hold values from 0 to 7, each once
Outputs:
- sparse_codes: float32 [128, 8192], P(None, 'tm')
- dictionary: float32 [128, 36864], P(None, 'chan')
- residual: float32 [384, 8192], P('chan', 'tm')
Inputs may be any that keep to these rules, and one draw needn't show every extreme that they name: `plan`: every atom block from 0 to 7 appears exactly once.
All inputs are finite; a program needn't handle non-finite values.
Results may differ from a plain program's by a relative error of at most 0.013.
Values may be sent and summed in bfloat16 or wider, within the bound.
A program may use at most 64 MiB of HBM per device.

v0:
```python
import functools

import jax
import jax.numpy as jnp
from jax import lax
from jax.experimental import pallas as pl
from jax.experimental.pallas import tpu as pltpu
from jax.sharding import PartitionSpec as P

C = 384
K = 128
L = 96
BLOCK_ATOMS = 16
INNER = 2
OUTER = 2
CHANS = 96
SEG = 128
ENTRIES = C * L

code_rate = 0.3
move_rate = 0.5
tiny_eps = 1e-06

MESH = pl.DeviceIdType.MESH
F32 = jnp.float32
BF16 = jnp.bfloat16

OWN = 288
ROWS = 608
PLANE = 8
HALO = (
    (1, 0, 128, 160),
    (2, 0, 128, 32),
    (3, 96, 32, 0),
    (-1, 0, 128, 416),
    (-2, 0, 64, 544),
)
SIGNAL_HALO = (
    (1, 0, 128, 160),
    (2, 64, 64, 96),
    (-1, 0, 128, 416),
    (-2, 0, 64, 544),
)


def dot(a, b):
    return lax.dot_general(a, b, (((1,), (0,)), ((), ())), preferred_element_type=F32)


def dot_t(a, b):
    return lax.dot_general(a, b, (((1,), (1,)), ((), ())), preferred_element_type=F32)


def kernel(
    segments,
    plan_ref,
    dt_ref,
    codes_ref,
    signal_ref,
    thr_ref,
    codes_out,
    resid_out,
    dt_out,
    zst,
    zsend,
    sgx,
    sgown,
    rst,
    zp,
    rp,
    wb,
    wat,
    acc,
    sx,
    sx2,
    rx1,
    rx2,
    a16,
    gfull,
    gsend,
    grecv,
    zbuf,
    agbuf,
    old,
    new,
    pick,
    strecv,
    h_send,
    h_recv,
    s_send,
    s_recv,
    c_send,
    c_recv,
    p_send,
    p_recv,
    z_send,
    z_recv,
    a_send,
    a_recv,
    t_send,
    t_recv,
    keep_sem,
):
    unit = ENTRIES ** (-0.5)
    tm = lax.axis_index("tm")
    chan = lax.axis_index("chan")
    depth = segments // PLANE
    place = tm % PLANE
    level = tm // PLANE

    def seg(d):
        return (tm + d + segments) % segments

    def in_plane(d):
        return level * PLANE + (place + d) % PLANE

    def in_depth(d):
        return ((level + d) % depth) * PLANE + place

    partner = chan + 1 - 2 * (chan % 2)
    opposite = (chan + 2) % 4

    zsend[0] = codes_ref[...].T
    zst[0, OWN : OWN + SEG] = zsend[0]
    low = jnp.concatenate(
        [signal_ref[...].astype(F32), jnp.zeros((SEG - CHANS, SEG), F32)], axis=0
    ).T.astype(BF16)
    sgown[...] = low
    sgx[OWN : OWN + SEG] = low

    keep = pltpu.make_async_copy(dt_ref, dt_out, keep_sem)
    keep.start()

    def pick_body(o, carry):
        tall = lax.broadcasted_iota(jnp.int32, (1024, 128), 0)
        wide = lax.broadcasted_iota(jnp.int32, (1024, 128), 1)
        block = plan_ref[o]
        hit = ((tall // 128 + block) % 8 == wide // 16) & (
            tall % 128 == wide % 16 + block * BLOCK_ATOMS
        )
        pick[o] = jnp.where(hit, 1.0, 0.0).astype(BF16)
        return carry

    lax.fori_loop(0, OUTER, pick_body, 0)

    barrier = pltpu.get_barrier_semaphore()
    peers = [{"tm": seg(d)} for d in (-3, -2, -1, 1, 2, 3)]
    peers += [{"chan": (chan + d) % 4} for d in range(1, 4)]
    peers += [{"tm": in_plane(d)} for d in range(1, PLANE)]
    peers += [{"tm": in_depth(d)} for d in range(1, depth)]
    for peer in peers:
        pl.semaphore_signal(barrier, inc=1, device_id=peer, device_id_type=MESH)
    pl.semaphore_wait(barrier, len(peers))

    def remote(src, dst, send, recv, peer):
        return pltpu.make_async_remote_copy(
            src_ref=src,
            dst_ref=dst,
            send_sem=send,
            recv_sem=recv,
            device_id=peer,
            device_id_type=MESH,
        )

    def halo_copies(o):
        return [
            remote(
                zsend.at[o, pl.ds(first, rows)],
                zst.at[o, pl.ds(land, rows)],
                h_send.at[o, i],
                h_recv.at[o, i],
                {"tm": seg(d)},
            )
            for i, (d, first, rows, land) in enumerate(HALO)
        ]

    signal_copies = [
        remote(
            sgown.at[pl.ds(first, rows)],
            sgx.at[pl.ds(land, rows)],
            s_send.at[i],
            s_recv.at[i],
            {"tm": seg(d)},
        )
        for i, (d, first, rows, land) in enumerate(SIGNAL_HALO)
    ]
    halo = halo_copies(0)
    for copy in halo + signal_copies:
        copy.start()

    for q in range(3):
        for s in range(16):
            wb[q, s * 128 + CHANS : (s + 1) * 128] = jnp.zeros((128 - CHANS, 256), BF16)
        for j in range(2):
            wat[q, j * 128 + CHANS : (j + 1) * 128] = jnp.zeros((128 - CHANS, 2048), BF16)
    lane_block = lax.broadcasted_iota(jnp.int32, (CHANS, 128), 1) // BLOCK_ATOMS

    def arrange(i, carry):
        j, q = i // 3, i % 3
        here = pl.multiple_of(j * 128, 128)
        for half in range(2):
            found = [jnp.zeros((CHANS, 128), F32)] * OUTER
            for k in range(8):
                s = half * 8 + k
                value = dt_ref[pl.ds(16 * i + s, CHANS, stride=L), :]
                low = value.astype(BF16)
                wb[q, s * 128 : s * 128 + CHANS, pl.ds(here, 128)] = low
                wat[q, pl.ds(here, CHANS), s * 128 : (s + 1) * 128] = low
                turned = pltpu.roll(value, 16 * k, 1) if k else value
                found = [
                    jnp.where(lane_block == (plan_ref[o] + k) % 8, turned, found[o])
                    for o in range(OUTER)
                ]
            group = pl.ds(pl.multiple_of(i * 256 + half * 128, 128), 128)
            for o in range(OUTER):
                old[o, :, group] = found[o]
        return carry

    lax.fori_loop(0, 6, arrange, 0)

    for copy in halo + signal_copies:
        copy.wait()

    def in_window(a, b):
        when = tm * SEG - OWN + a + lax.broadcasted_iota(jnp.int32, (b - a, 1), 0)
        return when

    def clear_early(o):
        zst[o, 0:OWN] = jnp.where(in_window(0, OWN) >= 0, zst[o, 0:OWN], 0.0)

    def residual_rows(o, a, b):
        top = a - 80
        for s in range(16):
            zp[top:b, s * 128 : (s + 1) * 128] = zst[o, pl.ds(top - s, b - top), :].astype(BF16)
        n = b - a + 48
        acc[0:n] = jnp.zeros((n, 256), F32)

        def body(q, carry):
            acc[0:n] += dot_t(zp[pl.ds(pl.multiple_of(a - 48 - 16 * q, 16), n), :], wat[q])
            return carry

        lax.fori_loop(0, 3, body, 0)
        made = unit * (acc[48:n, 0:128] + acc[0 : n - 48, 128:256])
        value = sgx[a:b].astype(F32) - made
        rst[a:b] = jnp.where(in_window(a, b) < segments * SEG, value, 0.0)

    def score_rows(a, b):
        end = b + 80
        for s in range(16):
            rp[a:end, s * 128 : (s + 1) * 128] = rst[pl.ds(a + s, end - a), :].astype(BF16)
        n = b - a + 48
        acc[0:n] = jnp.zeros((n, 256), F32)

        def body(q, carry):
            acc[0:n] += dot(rp[pl.ds(pl.multiple_of(a + 16 * q, 16), n), :], wb[q])
            return carry

        lax.fori_loop(0, 3, body, 0)
        return unit * (acc[0 : n - 48, 0:128] + acc[48:n, 128:256])

    def update_rows(o, step, a, b):
        n = b - a
        i = o * INNER + step
        sx[0:n] = score_rows(a, b).astype(BF16)
        near = remote(
            sx.at[pl.ds(0, n)],
            rx1.at[i, pl.ds(0, n)],
            c_send.at[i, 0],
            c_recv.at[i, 0],
            {"chan": partner},
        )
        near.start()
        near.wait()
        sx2[0:n] = (sx[0:n].astype(F32) + rx1[i, 0:n].astype(F32)).astype(BF16)
        far = remote(
            sx2.at[pl.ds(0, n)],
            rx2.at[i, pl.ds(0, n)],
            c_send.at[i, 1],
            c_recv.at[i, 1],
            {"chan": opposite},
        )
        far.start()
        far.wait()
        scores = sx2[0:n].astype(F32) + rx2[i, 0:n].astype(F32)
        stepped = zst[o, a:b] + code_rate * scores
        limit = thr_ref[...]
        value = stepped - jnp.clip(stepped, -limit, limit)
        zst[o, a:b] = jnp.where(in_window(a, b) >= 0, value, 0.0)

    def lanes_sum(row):
        total = row[:, 0:128] + row[:, 128:256] + row[:, 256:384]
        total = jnp.broadcast_to(total, (8, 128))
        for shift in (64, 32, 16):
            total = total + pltpu.roll(total, shift, 1)
        return total

    def old_piece(o, piece):
        top, left = piece // 4 * 48, piece % 4 * 384
        return old[o, top : top + 48, left : left + 384]

    def three(row):
        return jnp.concatenate([row[0:1]] * 3, axis=1)

    def renew(o):
        turned = rst[OWN : OWN + SEG].T
        resid_out[...] = turned[0:CHANS]
        for half in range(2):
            lanes = slice(half * 128, half * 128 + 128)
            a16[:, lanes] = dot(
                zp[OWN - 80 : OWN + SEG, half * 1024 : half * 1024 + 1024],
                pick[o],
            ).astype(BF16)
        across_time = turned[0:CHANS].astype(BF16)
        for q in range(6):
            gfull[:, q * 256 : (q + 1) * 256] = dot(
                across_time, a16[80 - 16 * q : 208 - 16 * q, :]
            ).astype(BF16)
        for piece in range(PLANE):
            top, left = piece // 4 * 48, piece % 4 * 384
            gsend[piece] = gfull[top : top + 48, left : left + 384]
        copies = [
            remote(
                gsend.at[(place + d) % PLANE],
                grecv.at[o, d],
                p_send.at[o, d],
                p_recv.at[o, d],
                {"tm": in_plane(d)},
            )
            for d in range(1, PLANE)
        ]
        for copy in copies:
            copy.start()
        total = gsend[place].astype(F32)
        for d, copy in enumerate(copies, 1):
            copy.wait_recv()
            total = total + grecv[o, d].astype(F32)
        zbuf[o, level] = total.astype(BF16)
        sent = copies
        copies = [
            remote(
                zbuf.at[o, level],
                zbuf.at[o, level],
                z_send.at[o, d],
                z_recv.at[o, d],
                {"tm": in_depth(d)},
            )
            for d in range(1, depth)
        ]
        for copy in copies:
            copy.start()
        for copy in copies:
            copy.wait_recv()
        sent = sent + copies
        total = zbuf[o, 0].astype(F32)
        for i in range(1, depth):
            total = total + zbuf[o, i].astype(F32)
        agbuf[o, place] = total.astype(BF16)
        copies = [
            remote(
                agbuf.at[o, place],
                agbuf.at[o, place],
                a_send.at[o, d],
                a_recv.at[o, d],
                {"tm": in_plane(d)},
            )
            for d in range(1, PLANE)
        ]
        for copy in copies:
            copy.start()
        for copy in copies:
            copy.wait_recv()
        sent = sent + copies

        with_old = jnp.zeros((1, 384), F32)
        old_old = jnp.zeros((1, 384), F32)
        for piece in range(PLANE):
            grad, was = agbuf[o, piece].astype(F32), old_piece(o, piece)
            with_old = with_old + jnp.sum(grad * was, axis=0, keepdims=True)
            old_old = old_old + jnp.sum(was * was, axis=0, keepdims=True)
        with_old, old_old = lanes_sum(with_old), lanes_sum(old_old)
        own_coef = jnp.where(old_old > 0.0, with_old / jnp.maximum(old_old, 1e-30), 0.0)
        left_over = jnp.zeros((1, 384), F32)
        coef = three(own_coef)
        for piece in range(PLANE):
            part = agbuf[o, piece].astype(F32) - coef * old_piece(o, piece)
            left_over = left_over + jnp.sum(part * part, axis=0, keepdims=True)
        left_over = lanes_sum(left_over)
        row = lax.broadcasted_iota(jnp.int32, (8, 128), 0)
        packed = jnp.where(row == 0, with_old, jnp.where(row == 1, old_old, left_over))
        strecv[o, chan] = packed
        copies = [
            remote(
                strecv.at[o, chan],
                strecv.at[o, chan],
                t_send.at[o, d],
                t_recv.at[o, d],
                {"chan": (chan + d) % 4},
            )
            for d in range(1, 4)
        ]
        for copy in copies:
            copy.start()
        for copy in copies:
            copy.wait_recv()
        sent = sent + copies
        parts = [strecv[o, i] for i in range(4)]
        gd = [part[0:1] for part in parts]
        dd = [part[1:2] for part in parts]
        rr = [part[2:3] for part in parts]
        mean_sq = (dd[0] + dd[1] + dd[2] + dd[3]) / ENTRIES + tiny_eps
        along = (gd[0] + gd[1] + gd[2] + gd[3]) / ENTRIES / mean_sq
        spread = jnp.zeros((1, 128), F32)
        for i in range(4):
            mine = jnp.where(dd[i] > 0.0, gd[i] / jnp.maximum(dd[i], 1e-30), 0.0)
            off = mine - along
            spread = spread + rr[i] + off * (off * dd[i] + 2.0 * (gd[i] - mine * dd[i]))
        spread = jnp.maximum(spread, 0.0) / ENTRIES + tiny_eps
        along_row = three(along)
        gain = three(move_rate / jnp.sqrt(spread))
        shrink = three(1.0 / jnp.sqrt(mean_sq + 0.25))
        for piece in range(PLANE):
            was = old_piece(o, piece)
            across = agbuf[o, piece].astype(F32) - along_row * was
            top, left = piece // 4 * 48, piece % 4 * 384
            new[top : top + 48, left : left + 384] = (was + gain * across) * shrink
        for copy in sent:
            copy.wait_send()

    def place_block(o, arranged):
        mine = lane_block == plan_ref[o]

        def body(i, carry):
            j, q = i // 3, i % 3
            here = pl.multiple_of(j * 128, 128)
            for half in range(2):
                value = new[:, pl.ds(pl.multiple_of(i * 256 + half * 128, 128), 128)]
                for k in range(8):
                    s = half * 8 + k
                    taps = pl.ds(16 * i + s, CHANS, stride=L)
                    turned = pltpu.roll(value, 128 - 16 * k, 1) if k else value
                    merged = jnp.where(mine, turned, dt_out[taps, :])
                    dt_out[taps, :] = merged
                    if arranged:
                        low = merged.astype(BF16)
                        wb[q, s * 128 : s * 128 + CHANS, pl.ds(here, 128)] = low
                        wat[q, pl.ds(here, CHANS), s * 128 : (s + 1) * 128] = low
            return carry

        lax.fori_loop(0, 6, body, 0)

    keep.wait()

    def outer(o, carry):
        clear_early(o)
        residual_rows(o, 96, 608)
        update_rows(o, 0, 96, 512)
        residual_rows(o, 192, 512)
        update_rows(o, 1, 192, 416)

        @pl.when(o < OUTER - 1)
        def _():
            zsend[1] = zst[0, OWN : OWN + SEG]
            zst[1, OWN : OWN + SEG] = zst[0, OWN : OWN + SEG]
            for copy in halo_copies(1):
                copy.start()

        residual_rows(o, 288, 416)
        renew(o)

        @pl.when(o < OUTER - 1)
        def _():
            place_block(0, True)
            for copy in halo_copies(1):
                copy.wait()

        return carry

    lax.fori_loop(0, OUTER, outer, 0)
    codes_out[...] = zst[OUTER - 1, OWN : OWN + SEG].T
    place_block(OUTER - 1, False)


def shards(segments, signal, codes_init, dictionary_init, threshold, plan):
    turned = dictionary_init.T
    depth = segments // PLANE
    vmem = pl.BlockSpec(memory_space=pltpu.VMEM)
    dma = pltpu.SemaphoreType.DMA
    codes, resid, dt = pl.pallas_call(
        functools.partial(kernel, segments),
        out_shape=(
            jax.ShapeDtypeStruct((K, SEG), F32),
            jax.ShapeDtypeStruct((CHANS, SEG), F32),
            jax.ShapeDtypeStruct((CHANS * L, K), F32),
        ),
        in_specs=[pl.BlockSpec(memory_space=pltpu.SMEM)] + [vmem] * 4,
        out_specs=(vmem, vmem, vmem),
        scratch_shapes=[
            pltpu.VMEM((OUTER, ROWS, 128), F32),
            pltpu.VMEM((OUTER, SEG, 128), F32),
            pltpu.VMEM((ROWS, 128), BF16),
            pltpu.VMEM((SEG, 128), BF16),
            pltpu.VMEM((ROWS, 128), F32),
            pltpu.VMEM((ROWS, 2048), BF16),
            pltpu.VMEM((ROWS, 2048), BF16),
            pltpu.VMEM((3, 2048, 256), BF16),
            pltpu.VMEM((3, 256, 2048), BF16),
            pltpu.VMEM((560, 256), F32),
            pltpu.VMEM((416, 128), BF16),
            pltpu.VMEM((416, 128), BF16),
            pltpu.VMEM((4, 416, 128), BF16),
            pltpu.VMEM((4, 416, 128), BF16),
            pltpu.VMEM((208, 256), BF16),
            pltpu.VMEM((CHANS, 1536), BF16),
            pltpu.VMEM((PLANE, 48, 384), BF16),
            pltpu.VMEM((OUTER, PLANE, 48, 384), BF16),
            pltpu.VMEM((OUTER, depth, 48, 384), BF16),
            pltpu.VMEM((OUTER, PLANE, 48, 384), BF16),
            pltpu.VMEM((OUTER, CHANS, 1536), F32),
            pltpu.VMEM((CHANS, 1536), F32),
            pltpu.VMEM((OUTER, 1024, 128), BF16),
            pltpu.VMEM((OUTER, 4, 8, 128), F32),
            dma((OUTER, 5)),
            dma((OUTER, 5)),
            dma((4,)),
            dma((4,)),
            dma((4, 2)),
            dma((4, 2)),
            dma((OUTER, PLANE)),
            dma((OUTER, PLANE)),
            dma((OUTER, depth)),
            dma((OUTER, depth)),
            dma((OUTER, PLANE)),
            dma((OUTER, PLANE)),
            dma((OUTER, 4)),
            dma((OUTER, 4)),
            dma,
        ],
        compiler_params=pltpu.CompilerParams(
            collective_id=0, has_side_effects=True, vmem_limit_bytes=60 * 1024 * 1024
        ),
    )(plan, turned, codes_init, signal, threshold[None, :])
    return codes, dt.T, resid


def solution(mesh):
    placed = (P("chan", "tm"), P(None, "tm"), P(None, "chan"), P(), P())
    return jax.shard_map(
        functools.partial(shards, mesh.shape["tm"]),
        mesh=mesh,
        in_specs=placed,
        out_specs=(P(None, "tm"), P(None, "chan"), P("chan", "tm")),
        check_vma=False,
    )
```

profile of v0, /device:TPU:1, one launch (start us, length us, event | category | flops | bytes accessed | tf_op | source)
XLA Modules:
  0.0 145.7 jit_solution(12748603648370387528)
XLA Ops:
  0.6 6.0 %copy.8 = f32[128,9216]{0,1:T(8,128)} copy(f32[128,9216]{1,0:T(8,128)} %param.7) | data formatting | bytes 9437184 | tf_op args[2]
  6.7 131.6 %shard_map.76 = (f32[128,128]{1,0:T(8,128)}, f32[96,128]{1,0:T(8,128)}, f32[9216,128]{1,0:T(8,128)}) custom-call(s32[8]{0:T(128)} %plan_ref.1, f32[9216,128]{1,0:T(8,128)} %bitcast.3, f32[128,128]{1,0:T(8,128)} %codes_ref.1, bf16[96,128]{1,0:T(8,128)(2,1)} %signal_ref.1, f32[1,128]{1,0:T(1,128)} %bitcast.5), custom_call_target="tpu_custom_call" | custom-call | tf_op jit(solution)/shard_map/pallas_call | solution.py:488
  138.3 0.0 copy-start
  138.3 0.0 copy-start.1
  138.3 6.1 %copy.9 = f32[128,9216]{1,0:T(8,128)} copy(f32[128,9216]{0,1:T(8,128)} %bitcast.4) | data formatting | bytes 9437184
  144.4 0.0 copy-done
  144.4 0.6 copy.12
  145.0 0.0 copy-done.1
  145.0 0.6 copy.13
Async XLA Ops:
  138.3 6.1 %copy-start = (f32[128,128]{1,0:T(8,128)S(1)}, f32[128,128]{1,0:T(8,128)}, u32[]{:S(2)}) copy-start(f32[128,128]{1,0:T(8,128)} %get-tuple-element.15) | copy-start | bytes 196612
  138.3 6.7 %copy-start.1 = (f32[96,128]{1,0:T(8,128)S(1)}, f32[96,128]{1,0:T(8,128)}, u32[]{:S(2)}) copy-start(f32[96,128]{1,0:T(8,128)} %get-tuple-element.17) | copy-start | bytes 147460
where the time goes:
time: 146 us
  Pallas kernels  132 us (90%)
  local copies, waits for them, and re-layouts  13.4 us (9%)
    pallas_call x1, Pallas kernels, shards(): pl.pallas_call(functools.partial(kernel, segments), out_shape=(jax.ShapeD...  132 us
    unnamed x8, local copies, waits for them, and re-layouts  13.4 us

commit v1 on v0

--- a/solution.py
+++ b/solution.py
@@ -54,7 +54,7 @@
 def kernel(
     segments,
     plan_ref,
-    dt_ref,
+    dt_hbm,
     codes_ref,
     signal_ref,
     thr_ref,
@@ -84,6 +84,8 @@
     old,
     new,
     pick,
+    dt_ref,
+    by_lag,
     strecv,
     h_send,
     h_recv,
@@ -99,7 +101,7 @@
     a_recv,
     t_send,
     t_recv,
-    keep_sem,
+    load_sem,
 ):
     unit = ENTRIES ** (-0.5)
     tm = lax.axis_index("tm")
@@ -120,6 +122,8 @@
     partner = chan + 1 - 2 * (chan % 2)
     opposite = (chan + 2) % 4
 
+    load = pltpu.make_async_copy(dt_hbm, dt_ref, load_sem)
+    load.start()
     zsend[0] = codes_ref[...].T
     zst[0, OWN : OWN + SEG] = zsend[0]
     low = jnp.concatenate(
@@ -128,8 +132,6 @@
     sgown[...] = low
     sgx[OWN : OWN + SEG] = low
 
-    keep = pltpu.make_async_copy(dt_ref, dt_out, keep_sem)
-    keep.start()
 
     def pick_body(o, carry):
         tall = lax.broadcasted_iota(jnp.int32, (1024, 128), 0)
@@ -193,6 +195,7 @@
             wb[q, s * 128 + CHANS : (s + 1) * 128] = jnp.zeros((128 - CHANS, 256), BF16)
         for j in range(2):
             wat[q, j * 128 + CHANS : (j + 1) * 128] = jnp.zeros((128 - CHANS, 2048), BF16)
+    load.wait()
     lane_block = lax.broadcasted_iota(jnp.int32, (CHANS, 128), 1) // BLOCK_ATOMS
 
     def arrange(i, carry):
@@ -203,6 +206,7 @@
             for k in range(8):
                 s = half * 8 + k
                 value = dt_ref[pl.ds(16 * i + s, CHANS, stride=L), :]
+                by_lag[16 * i + s] = value
                 low = value.astype(BF16)
                 wb[q, s * 128 : s * 128 + CHANS, pl.ds(here, 128)] = low
                 wat[q, pl.ds(here, CHANS), s * 128 : (s + 1) * 128] = low
@@ -244,48 +248,58 @@
         value = sgx[a:b].astype(F32) - made
         rst[a:b] = jnp.where(in_window(a, b) < segments * SEG, value, 0.0)
 
-    def score_rows(a, b):
+    def update_rows(o, step, a, b):
+        n, i = b - a, o * INNER + step
+        half = n // 2
         end = b + 80
         for s in range(16):
             rp[a:end, s * 128 : (s + 1) * 128] = rst[pl.ds(a + s, end - a), :].astype(BF16)
-        n = b - a + 48
-        acc[0:n] = jnp.zeros((n, 256), F32)
-
-        def body(q, carry):
-            acc[0:n] += dot(rp[pl.ds(pl.multiple_of(a + 16 * q, 16), n), :], wb[q])
-            return carry
-
-        lax.fori_loop(0, 3, body, 0)
-        return unit * (acc[0 : n - 48, 0:128] + acc[48:n, 128:256])
-
-    def update_rows(o, step, a, b):
-        n = b - a
-        i = o * INNER + step
-        sx[0:n] = score_rows(a, b).astype(BF16)
-        near = remote(
-            sx.at[pl.ds(0, n)],
-            rx1.at[i, pl.ds(0, n)],
-            c_send.at[i, 0],
-            c_recv.at[i, 0],
-            {"chan": partner},
-        )
-        near.start()
-        near.wait()
-        sx2[0:n] = (sx[0:n].astype(F32) + rx1[i, 0:n].astype(F32)).astype(BF16)
-        far = remote(
-            sx2.at[pl.ds(0, n)],
-            rx2.at[i, pl.ds(0, n)],
-            c_send.at[i, 1],
-            c_recv.at[i, 1],
-            {"chan": opposite},
-        )
-        far.start()
-        far.wait()
-        scores = sx2[0:n].astype(F32) + rx2[i, 0:n].astype(F32)
-        stepped = zst[o, a:b] + code_rate * scores
+        near, far = [], []
+        for part, (first, last) in enumerate(((0, half + 48), (half + 48, n + 48))):
+            rows = last - first
+            acc[first:last] = jnp.zeros((rows, 256), F32)
+
+            def body(q, carry):
+                start = pl.multiple_of(a + first + 16 * q, 16)
+                acc[first:last] += dot(rp[pl.ds(start, rows), :], wb[q])
+                return carry
+
+            lax.fori_loop(0, 3, body, 0)
+            low, high = part * half, (part + 1) * half
+            scores = unit * (acc[low:high, 0:128] + acc[low + 48 : high + 48, 128:256])
+            sx[low:high] = scores.astype(BF16)
+            copy = remote(
+                sx.at[pl.ds(low, half)],
+                rx1.at[i, pl.ds(low, half)],
+                c_send.at[i, 0, part],
+                c_recv.at[i, 0, part],
+                {"chan": partner},
+            )
+            copy.start()
+            near.append(copy)
+        for part in range(2):
+            low, high = part * half, (part + 1) * half
+            near[part].wait()
+            sx2[low:high] = (
+                sx[low:high].astype(F32) + rx1[i, pl.ds(low, half)].astype(F32)
+            ).astype(BF16)
+            copy = remote(
+                sx2.at[pl.ds(low, half)],
+                rx2.at[i, pl.ds(low, half)],
+                c_send.at[i, 1, part],
+                c_recv.at[i, 1, part],
+                {"chan": opposite},
+            )
+            copy.start()
+            far.append(copy)
         limit = thr_ref[...]
-        value = stepped - jnp.clip(stepped, -limit, limit)
-        zst[o, a:b] = jnp.where(in_window(a, b) >= 0, value, 0.0)
+        for part in range(2):
+            low, high = part * half, (part + 1) * half
+            far[part].wait()
+            scores = sx2[low:high].astype(F32) + rx2[i, pl.ds(low, half)].astype(F32)
+            stepped = zst[o, a + low : a + high] + code_rate * scores
+            value = stepped - jnp.clip(stepped, -limit, limit)
+            zst[o, a + low : a + high] = jnp.where(in_window(a + low, a + high) >= 0, value, 0.0)
 
     def lanes_sum(row):
         total = row[:, 0:128] + row[:, 128:256] + row[:, 256:384]
@@ -318,58 +332,62 @@
         for piece in range(PLANE):
             top, left = piece // 4 * 48, piece % 4 * 384
             gsend[piece] = gfull[top : top + 48, left : left + 384]
-        copies = [
-            remote(
-                gsend.at[(place + d) % PLANE],
-                grecv.at[o, d],
-                p_send.at[o, d],
-                p_recv.at[o, d],
-                {"tm": in_plane(d)},
+        sent = []
+
+        def spread_rows(part, peers, source, target, send, recv):
+            rows = pl.ds(part * 16, 16)
+            copies = [
+                remote(
+                    source(d).at[rows],
+                    target(d).at[rows],
+                    send.at[o, d, part],
+                    recv.at[o, d, part],
+                    {"tm": peer},
+                )
+                for d, peer in peers
+            ]
+            for copy in copies:
+                copy.start()
+            sent.extend(copies)
+            return copies
+
+        plane = [(d, in_plane(d)) for d in range(1, PLANE)]
+        levels = [(d, in_depth(d)) for d in range(1, depth)]
+        scatter = [
+            spread_rows(
+                part,
+                plane,
+                lambda d: gsend.at[(place + d) % PLANE],
+                lambda d: grecv.at[o, d],
+                p_send,
+                p_recv,
             )
-            for d in range(1, PLANE)
+            for part in range(3)
         ]
-        for copy in copies:
-            copy.start()
-        total = gsend[place].astype(F32)
-        for d, copy in enumerate(copies, 1):
-            copy.wait_recv()
-            total = total + grecv[o, d].astype(F32)
-        zbuf[o, level] = total.astype(BF16)
-        sent = copies
-        copies = [
-            remote(
-                zbuf.at[o, level],
-                zbuf.at[o, level],
-                z_send.at[o, d],
-                z_recv.at[o, d],
-                {"tm": in_depth(d)},
-            )
-            for d in range(1, depth)
-        ]
-        for copy in copies:
-            copy.start()
-        for copy in copies:
-            copy.wait_recv()
-        sent = sent + copies
-        total = zbuf[o, 0].astype(F32)
-        for i in range(1, depth):
-            total = total + zbuf[o, i].astype(F32)
-        agbuf[o, place] = total.astype(BF16)
-        copies = [
-            remote(
-                agbuf.at[o, place],
-                agbuf.at[o, place],
-                a_send.at[o, d],
-                a_recv.at[o, d],
-                {"tm": in_plane(d)},
-            )
-            for d in range(1, PLANE)
-        ]
-        for copy in copies:
-            copy.start()
-        for copy in copies:
-            copy.wait_recv()
-        sent = sent + copies
+        across_levels = []
+        for part in range(3):
+            rows = pl.ds(part * 16, 16)
+            total = gsend[place, rows].astype(F32)
+            for d, copy in enumerate(scatter[part], 1):
+                copy.wait_recv()
+                total = total + grecv[o, d, rows].astype(F32)
+            zbuf[o, level, rows] = total.astype(BF16)
+            slot = lambda d: zbuf.at[o, level]
+            across_levels.append(spread_rows(part, levels, slot, slot, z_send, z_recv))
+        gather = []
+        for part in range(3):
+            rows = pl.ds(part * 16, 16)
+            for copy in across_levels[part]:
+                copy.wait_recv()
+            total = zbuf[o, 0, rows].astype(F32)
+            for i in range(1, depth):
+                total = total + zbuf[o, i, rows].astype(F32)
+            agbuf[o, place, rows] = total.astype(BF16)
+            slot = lambda d: agbuf.at[o, place]
+            gather.append(spread_rows(part, plane, slot, slot, a_send, a_recv))
+        for copies in gather:
+            for copy in copies:
+                copy.wait_recv()
 
         with_old = jnp.zeros((1, 384), F32)
         old_old = jnp.zeros((1, 384), F32)
@@ -436,19 +454,18 @@
                 value = new[:, pl.ds(pl.multiple_of(i * 256 + half * 128, 128), 128)]
                 for k in range(8):
                     s = half * 8 + k
-                    taps = pl.ds(16 * i + s, CHANS, stride=L)
                     turned = pltpu.roll(value, 128 - 16 * k, 1) if k else value
-                    merged = jnp.where(mine, turned, dt_out[taps, :])
-                    dt_out[taps, :] = merged
-                    if arranged:
+                    merged = jnp.where(mine, turned, by_lag[16 * i + s])
+                    if not arranged:
+                        dt_out[pl.ds(16 * i + s, CHANS, stride=L), :] = merged
+                    else:
+                        by_lag[16 * i + s] = merged
                         low = merged.astype(BF16)
                         wb[q, s * 128 : s * 128 + CHANS, pl.ds(here, 128)] = low
                         wat[q, pl.ds(here, CHANS), s * 128 : (s + 1) * 128] = low
             return carry
 
         lax.fori_loop(0, 6, body, 0)
-
-    keep.wait()
 
     def outer(o, carry):
         clear_early(o)
@@ -492,7 +509,8 @@
             jax.ShapeDtypeStruct((CHANS, SEG), F32),
             jax.ShapeDtypeStruct((CHANS * L, K), F32),
         ),
-        in_specs=[pl.BlockSpec(memory_space=pltpu.SMEM)] + [vmem] * 4,
+        in_specs=[pl.BlockSpec(memory_space=pltpu.SMEM), pl.BlockSpec(memory_space=pl.ANY)]
+        + [vmem] * 3,
         out_specs=(vmem, vmem, vmem),
         scratch_shapes=[
             pltpu.VMEM((OUTER, ROWS, 128), F32),
@@ -518,19 +536,21 @@
             pltpu.VMEM((OUTER, CHANS, 1536), F32),
             pltpu.VMEM((CHANS, 1536), F32),
             pltpu.VMEM((OUTER, 1024, 128), BF16),
+            pltpu.VMEM((CHANS * L, K), F32),
+            pltpu.VMEM((L, CHANS, K), F32),
             pltpu.VMEM((OUTER, 4, 8, 128), F32),
             dma((OUTER, 5)),
             dma((OUTER, 5)),
             dma((4,)),
             dma((4,)),
-            dma((4, 2)),
-            dma((4, 2)),
-            dma((OUTER, PLANE)),
-            dma((OUTER, PLANE)),
-            dma((OUTER, depth)),
-            dma((OUTER, depth)),
-            dma((OUTER, PLANE)),
-            dma((OUTER, PLANE)),
+            dma((4, 2, 2)),
+            dma((4, 2, 2)),
+            dma((OUTER, PLANE, 3)),
+            dma((OUTER, PLANE, 3)),
+            dma((OUTER, depth, 3)),
+            dma((OUTER, depth, 3)),
+            dma((OUTER, PLANE, 3)),
+            dma((OUTER, PLANE, 3)),
             dma((OUTER, 4)),
             dma((OUTER, 4)),
             dma,

time: 146 us -> 134 us (0.918)
  Pallas kernels: 132 us -> 119 us
    pallas_call x1, Pallas kernels: 132 us -> 119 us  [shards(): pl.pallas_call(functools.partial(kernel, segments), out_shape=(jax.ShapeD...]
where the time goes in v1:
time: 134 us; the launch traced here: 133 us
  Pallas kernels  119 us (89%)
  local copies, waits for them, and re-layouts  13.4 us (10%)
    pallas_call x1, Pallas kernels, shards(): pl.pallas_call(functools.partial(kernel, segments), out_shape=(jax.ShapeD...  119 us
    unnamed x8, local copies, waits for them, and re-layouts  13.4 us

profile of v1, /device:TPU:1, one launch (start us, length us, event | category | flops | bytes accessed | tf_op | source)
XLA Modules:
  0.0 133.4 jit_solution(5187508199564419865)
XLA Ops:
  0.6 6.0 %copy.8 = f32[128,9216]{0,1:T(8,128)} copy(f32[128,9216]{1,0:T(8,128)} %param.7) | data formatting | bytes 9437184 | tf_op args[2]
  6.7 119.4 %shard_map.76 = (f32[128,128]{1,0:T(8,128)}, f32[96,128]{1,0:T(8,128)}, f32[9216,128]{1,0:T(8,128)}) custom-call(s32[8]{0:T(128)} %plan_ref.1, f32[9216,128]{1,0:T(8,128)} %bitcast.3, f32[128,128]{1,0:T(8,128)} %codes_ref.1, bf16[96,128]{1,0:T(8,128)(2,1)} %signal_ref.1, f32[1,128]{1,0:T(1,128)} %bitcast.5), custom_call_target="tpu_custom_call" | custom-call | tf_op jit(solution)/shard_map/pallas_call | solution.py:505
  126.1 0.0 copy-start
  126.1 0.0 copy-start.1
  126.1 6.1 %copy.9 = f32[128,9216]{1,0:T(8,128)} copy(f32[128,9216]{0,1:T(8,128)} %bitcast.4) | data formatting | bytes 9437184
  132.2 0.0 copy-done
  132.2 0.6 copy.12
  132.8 0.0 copy-done.1
  132.8 0.6 copy.13
Async XLA Ops:
  126.1 6.1 %copy-start = (f32[128,128]{1,0:T(8,128)S(1)}, f32[128,128]{1,0:T(8,128)}, u32[]{:S(2)}) copy-start(f32[128,128]{1,0:T(8,128)} %get-tuple-element.15) | copy-start | bytes 196612
  126.1 6.7 %copy-start.1 = (f32[96,128]{1,0:T(8,128)S(1)}, f32[96,128]{1,0:T(8,128)}, u32[]{:S(2)}) copy-start(f32[96,128]{1,0:T(8,128)} %get-tuple-element.17) | copy-start | bytes 147460

commit v2 on v1

--- a/solution.py
+++ b/solution.py
@@ -60,7 +60,8 @@
     thr_ref,
     codes_out,
     resid_out,
-    dt_out,
+    rows_first,
+    rows_last,
     zst,
     zsend,
     sgx,
@@ -85,7 +86,11 @@
     new,
     pick,
     dt_ref,
-    by_lag,
+    block_codes,
+    block_low,
+    by_tap,
+    in_order,
+    by_atom,
     strecv,
     h_send,
     h_recv,
@@ -206,7 +211,6 @@
             for k in range(8):
                 s = half * 8 + k
                 value = dt_ref[pl.ds(16 * i + s, CHANS, stride=L), :]
-                by_lag[16 * i + s] = value
                 low = value.astype(BF16)
                 wb[q, s * 128 : s * 128 + CHANS, pl.ds(here, 128)] = low
                 wat[q, pl.ds(here, CHANS), s * 128 : (s + 1) * 128] = low
@@ -232,18 +236,16 @@
     def clear_early(o):
         zst[o, 0:OWN] = jnp.where(in_window(0, OWN) >= 0, zst[o, 0:OWN], 0.0)
 
-    def residual_rows(o, a, b):
+    def convolve_rows(o, a, b):
         top = a - 80
         for s in range(16):
             zp[top:b, s * 128 : (s + 1) * 128] = zst[o, pl.ds(top - s, b - top), :].astype(BF16)
+        total = dot_t(zp[a - 48 : b, :], wat[0])
+        total = total + dot_t(zp[a - 64 : b - 16, :], wat[1])
+        acc[0 : b - a + 48] = total + dot_t(zp[a - 80 : b - 32, :], wat[2])
+
+    def residual_rows(a, b):
         n = b - a + 48
-        acc[0:n] = jnp.zeros((n, 256), F32)
-
-        def body(q, carry):
-            acc[0:n] += dot_t(zp[pl.ds(pl.multiple_of(a - 48 - 16 * q, 16), n), :], wat[q])
-            return carry
-
-        lax.fori_loop(0, 3, body, 0)
         made = unit * (acc[48:n, 0:128] + acc[0 : n - 48, 128:256])
         value = sgx[a:b].astype(F32) - made
         rst[a:b] = jnp.where(in_window(a, b) < segments * SEG, value, 0.0)
@@ -256,15 +258,10 @@
             rp[a:end, s * 128 : (s + 1) * 128] = rst[pl.ds(a + s, end - a), :].astype(BF16)
         near, far = [], []
         for part, (first, last) in enumerate(((0, half + 48), (half + 48, n + 48))):
-            rows = last - first
-            acc[first:last] = jnp.zeros((rows, 256), F32)
-
-            def body(q, carry):
-                start = pl.multiple_of(a + first + 16 * q, 16)
-                acc[first:last] += dot(rp[pl.ds(start, rows), :], wb[q])
-                return carry
-
-            lax.fori_loop(0, 3, body, 0)
+            start, stop = a + first, a + last
+            total = dot(rp[start:stop, :], wb[0])
+            total = total + dot(rp[start + 16 : stop + 16, :], wb[1])
+            acc[first:last] = total + dot(rp[start + 32 : stop + 32, :], wb[2])
             low, high = part * half, (part + 1) * half
             scores = unit * (acc[low:high, 0:128] + acc[low + 48 : high + 48, 128:256])
             sx[low:high] = scores.astype(BF16)
@@ -364,6 +361,7 @@
             )
             for part in range(3)
         ]
+        cover(o)
         across_levels = []
         for part in range(3):
             rows = pl.ds(part * 16, 16)
@@ -440,38 +438,99 @@
             was = old_piece(o, piece)
             across = agbuf[o, piece].astype(F32) - along_row * was
             top, left = piece // 4 * 48, piece % 4 * 384
-            new[top : top + 48, left : left + 384] = (was + gain * across) * shrink
+            value = (was + gain * across) * shrink
+            new[o, top : top + 48, left : left + 384] = value
+            block_low[0, top : top + 48, left : left + 384] = value.astype(BF16)
         for copy in sent:
             copy.wait_send()
 
-    def place_block(o, arranged):
-        mine = lane_block == plan_ref[o]
+    def place_block(o):
+        mine = jnp.where(lane_block == plan_ref[o], 1.0, 0.0)
+        others = (1.0 - mine).astype(BF16)
 
         def body(i, carry):
             j, q = i // 3, i % 3
             here = pl.multiple_of(j * 128, 128)
             for half in range(2):
-                value = new[:, pl.ds(pl.multiple_of(i * 256 + half * 128, 128), 128)]
+                value = new[o, :, pl.ds(pl.multiple_of(i * 256 + half * 128, 128), 128)]
                 for k in range(8):
                     s = half * 8 + k
+                    rows = slice(s * 128, s * 128 + CHANS)
                     turned = pltpu.roll(value, 128 - 16 * k, 1) if k else value
-                    merged = jnp.where(mine, turned, by_lag[16 * i + s])
-                    if not arranged:
-                        dt_out[pl.ds(16 * i + s, CHANS, stride=L), :] = merged
-                    else:
-                        by_lag[16 * i + s] = merged
-                        low = merged.astype(BF16)
-                        wb[q, s * 128 : s * 128 + CHANS, pl.ds(here, 128)] = low
-                        wat[q, pl.ds(here, CHANS), s * 128 : (s + 1) * 128] = low
+                    low = wb[q, rows, pl.ds(here, 128)] * others + (turned * mine).astype(BF16)
+                    wb[q, rows, pl.ds(here, 128)] = low
+                    wat[q, pl.ds(here, CHANS), s * 128 : (s + 1) * 128] = low
             return carry
 
         lax.fori_loop(0, 6, body, 0)
 
+    def correct(which, sign):
+        total = None
+        for q in range(6):
+            part = dot_t(
+                block_codes[96 - 16 * q : ROWS - 16 * q, :],
+                block_low[which, :, q * 256 : (q + 1) * 256],
+            )
+            total = part if total is None else total + part
+        acc[48:560, 0:128] += sign * total
+
+    def write_rows(o):
+        rows_out = (rows_first, rows_last)[o]
+        block = jnp.zeros((BLOCK_ATOMS, 128), jnp.int32) + plan_ref[o]
+        bits = [block // step % 2 == 1 for step in (4, 2, 1)]
+        pad = jnp.zeros((128 - CHANS, 128), F32)
+        for g in range(12):
+            value = new[o, :, g * 128 : (g + 1) * 128]
+            by_tap[g * 128 : (g + 1) * 128] = jnp.concatenate([value, pad], axis=0).T
+        for g in range(12):
+            group = [by_tap[g * 128 + i * 16 : g * 128 + (i + 1) * 16] for i in range(8)]
+            for step, moved in zip((4, 2, 1), bits):
+                group = [jnp.where(moved, group[(i + step) % 8], group[i]) for i in range(8)]
+            for i in range(8):
+                in_order[g * 128 + i * 16 : g * 128 + (i + 1) * 16] = group[i]
+        for atom in range(BLOCK_ATOMS):
+            taps = in_order[pl.ds(atom, L, stride=BLOCK_ATOMS), :]
+            turned = jnp.concatenate([taps, pad], axis=0).T
+            by_atom[atom * 97 : atom * 97 + CHANS] = turned[0:CHANS]
+        lane = lax.broadcasted_iota(jnp.int32, (BLOCK_ATOMS, 128), 1)
+
+        def body(m, carry):
+            one = [by_atom[pl.ds(4 * m + r, BLOCK_ATOMS, stride=97), :] for r in range(4)]
+            one = [pltpu.roll(part, 96 * r % 128, 1) if r else part for r, part in enumerate(one)]
+            for t in range(3):
+                lanes = pl.ds(pl.multiple_of(m * 384 + t * 128, 128), 128)
+                rows_out[:, lanes] = jnp.where(lane < 96 - 32 * t, one[t], one[t + 1])
+            return carry
+
+        lax.fori_loop(0, 24, body, 0)
+
+    def cover(o):
+        @pl.when(o < OUTER - 1)
+        def _():
+            for copy in halo_copies(1):
+                copy.wait()
+            clear_early(1)
+            convolve_rows(1, 96, 608)
+            for half in range(2):
+                block_codes[16:ROWS, half * 128 : half * 128 + 128] = dot(
+                    zp[16:ROWS, half * 1024 : half * 1024 + 1024], pick[0]
+                ).astype(BF16)
+            block_low[1, 0:CHANS] = old[0].astype(BF16)
+            correct(1, -1.0)
+
+        @pl.when(o > 0)
+        def _():
+            write_rows(0)
+
+    block_low[:, CHANS:128] = jnp.zeros((2, 128 - CHANS, 1536), BF16)
+    clear_early(0)
+    convolve_rows(0, 96, 608)
+
     def outer(o, carry):
-        clear_early(o)
-        residual_rows(o, 96, 608)
+        residual_rows(96, 608)
         update_rows(o, 0, 96, 512)
-        residual_rows(o, 192, 512)
+        convolve_rows(o, 192, 512)
+        residual_rows(192, 512)
         update_rows(o, 1, 192, 416)
 
         @pl.when(o < OUTER - 1)
@@ -481,20 +540,20 @@
             for copy in halo_copies(1):
                 copy.start()
 
-        residual_rows(o, 288, 416)
+        convolve_rows(o, 288, 416)
+        residual_rows(288, 416)
         renew(o)
 
         @pl.when(o < OUTER - 1)
         def _():
-            place_block(0, True)
-            for copy in halo_copies(1):
-                copy.wait()
+            correct(0, 1.0)
+            place_block(0)
 
         return carry
 
     lax.fori_loop(0, OUTER, outer, 0)
     codes_out[...] = zst[OUTER - 1, OWN : OWN + SEG].T
-    place_block(OUTER - 1, False)
+    write_rows(OUTER - 1)
 
 
 def shards(segments, signal, codes_init, dictionary_init, threshold, plan):
@@ -502,16 +561,16 @@
     depth = segments // PLANE
     vmem = pl.BlockSpec(memory_space=pltpu.VMEM)
     dma = pltpu.SemaphoreType.DMA
-    codes, resid, dt = pl.pallas_call(
+    codes, resid, *rows = pl.pallas_call(
         functools.partial(kernel, segments),
         out_shape=(
             jax.ShapeDtypeStruct((K, SEG), F32),
             jax.ShapeDtypeStruct((CHANS, SEG), F32),
-            jax.ShapeDtypeStruct((CHANS * L, K), F32),
-        ),
+        )
+        + (jax.ShapeDtypeStruct((BLOCK_ATOMS, CHANS * L), F32),) * OUTER,
         in_specs=[pl.BlockSpec(memory_space=pltpu.SMEM), pl.BlockSpec(memory_space=pl.ANY)]
         + [vmem] * 3,
-        out_specs=(vmem, vmem, vmem),
+        out_specs=(vmem,) * 4,
         scratch_shapes=[
             pltpu.VMEM((OUTER, ROWS, 128), F32),
             pltpu.VMEM((OUTER, SEG, 128), F32),
@@ -534,10 +593,14 @@
             pltpu.VMEM((OUTER, depth, 48, 384), BF16),
             pltpu.VMEM((OUTER, PLANE, 48, 384), BF16),
             pltpu.VMEM((OUTER, CHANS, 1536), F32),
-            pltpu.VMEM((CHANS, 1536), F32),
+            pltpu.VMEM((OUTER, CHANS, 1536), F32),
             pltpu.VMEM((OUTER, 1024, 128), BF16),
             pltpu.VMEM((CHANS * L, K), F32),
-            pltpu.VMEM((L, CHANS, K), F32),
+            pltpu.VMEM((ROWS, 256), BF16),
+            pltpu.VMEM((2, 128, 1536), BF16),
+            pltpu.VMEM((1536, 128), F32),
+            pltpu.VMEM((1536, 128), F32),
+            pltpu.VMEM((16 * 97, 128), F32),
             pltpu.VMEM((OUTER, 4, 8, 128), F32),
             dma((OUTER, 5)),
             dma((OUTER, 5)),
@@ -559,7 +622,11 @@
             collective_id=0, has_side_effects=True, vmem_limit_bytes=60 * 1024 * 1024
         ),
     )(plan, turned, codes_init, signal, threshold[None, :])
-    return codes, dt.T, resid
+    dictionary = dictionary_init.reshape(K // BLOCK_ATOMS, BLOCK_ATOMS, CHANS * L)
+    block = jnp.arange(K // BLOCK_ATOMS)[:, None, None]
+    for o in range(OUTER):
+        dictionary = jnp.where(block == plan[o], rows[o], dictionary)
+    return codes, dictionary.reshape(K, CHANS * L), resid
 
 
 def solution(mesh):

time: 134 us -> 130 us (0.970)
  other arithmetic: 0 us -> 6.93 us
  Pallas kernels: 119 us -> 113 us
  local copies, waits for them, and re-layouts: 13.4 us -> 8.94 us
    unnamed x8 -> x7, local copies, waits for them, and re-layouts: 13.4 us -> 7.3 us
    pallas_call x1, Pallas kernels: 119 us -> 113 us  [shards(): pl.pallas_call(functools.partial(kernel, segments), out_shape=(jax.ShapeD...]
    select_n x0 -> x1, other arithmetic: none -> 5.63 us  [shards(): dictionary = jnp.where(block == plan[o], rows[o], dictionary)]
where the time goes in v2:
time: 130 us
  Pallas kernels  113 us (87%)
  local copies, waits for them, and re-layouts  8.94 us (7%)
  other arithmetic  6.93 us (5%)
    pallas_call x1, Pallas kernels, shards(): pl.pallas_call(functools.partial(kernel, segments), out_shape=(jax.ShapeD...  113 us
    unnamed x7, local copies, waits for them, and re-layouts  7.3 us
    select_n x1, other arithmetic, shards(): dictionary = jnp.where(block == plan[o], rows[o], dictionary)  5.63 us

profile of v2, /device:TPU:1, one launch (start us, length us, event | category | flops | bytes accessed | tf_op | source)
XLA Modules:
  0.0 129.9 jit_solution(16525513976631768995)
XLA Ops:
  0.6 1.3 %fusion.1 = (s32[1]{0:T(128)}, s32[1]{0:T(128)}) fusion(s32[8]{0:T(128)} %plan_ref.1), kind=kLoop, calls=%fused_computation.4 | loop fusion | bytes 16 | tf_op jit(solution)/shard_map/slice | solution.py:628
  1.9 0.6 iota_compare_fusion.1
  2.6 0.1 broadcast_in_dim.37
  2.7 0.1 broadcast_in_dim.38
  2.8 0.7 iota_compare_fusion
  3.4 0.1 broadcast_in_dim.42
  3.5 0.1 broadcast_in_dim.43
  3.6 6.0 %copy.8 = f32[128,9216]{0,1:T(8,128)} copy(f32[128,9216]{1,0:T(8,128)} %param.7) | data formatting | bytes 9437184 | tf_op args[2]
  9.6 113.4 %shard_map.76 = (f32[128,128]{1,0:T(8,128)}, f32[96,128]{1,0:T(8,128)}, f32[16,9216]{1,0:T(8,128)}, f32[16,9216]{1,0:T(8,128)}) custom-call(s32[8]{0:T(128)} %plan_ref.1, f32[9216,128]{1,0:T(8,128)} %bitcast.10, f32[128,128]{1,0:T(8,128)} %codes_ref.1, bf16[96,128]{1,0:T(8,128)(2,1)} %signal_ref.1, f32[1,128]{1,0:T(1,128)} %bitcast.11), custom_call_target="tpu_custom_call" | custom-call | tf_op jit(solution)/shard_map/pallas_call | solution.py:564
  123.0 0.0 copy-start
  123.0 0.0 copy-start.1
  123.0 5.6 %fusion = f32[128,9216]{1,0:T(8,128)} fusion(f32[128,9216]{1,0:T(8,128)} %param.7, f32[16,9216]{1,0:T(8,128)} %get-tuple-element.9, f32[16,9216]{1,0:T(8,128)} %get-tuple-element.8, pred[128]{0:T(512)(128)(4,1)S(1)} %broadcast_in_dim.43, pred[128]{0:T(512)(128)(4,1)S(1)} %broadcast_in_dim.38), kind=kLoop, calls=%fused_computation.1 | loop fusion | flops 2359296 | bytes 10617088 | tf_op jit(solution)/shard_map/jit(_where)/select_n | solution.py:628
  128.7 0.0 copy-done
  128.7 0.6 copy.11
  129.3 0.0 copy-done.1
  129.3 0.6 copy.12
Async XLA Ops:
  123.0 5.6 %copy-start = (f32[128,128]{1,0:T(8,128)S(1)}, f32[128,128]{1,0:T(8,128)}, u32[]{:S(2)}) copy-start(f32[128,128]{1,0:T(8,128)} %get-tuple-element.16) | copy-start | bytes 196612
  123.0 6.3 %copy-start.1 = (f32[96,128]{1,0:T(8,128)S(1)}, f32[96,128]{1,0:T(8,128)}, u32[]{:S(2)}) copy-start(f32[96,128]{1,0:T(8,128)} %get-tuple-element.18) | copy-start | bytes 147460

commit v3 on v2

--- a/solution.py
+++ b/solution.py
@@ -21,6 +21,7 @@
 move_rate = 0.5
 tiny_eps = 1e-06
 
+VMEM_LIMIT = 32 * 1024 * 1024
 MESH = pl.DeviceIdType.MESH
 F32 = jnp.float32
 BF16 = jnp.bfloat16
@@ -62,6 +63,7 @@
     resid_out,
     rows_first,
     rows_last,
+    owner_out,
     zst,
     zsend,
     sgx,
@@ -236,13 +238,15 @@
     def clear_early(o):
         zst[o, 0:OWN] = jnp.where(in_window(0, OWN) >= 0, zst[o, 0:OWN], 0.0)
 
-    def convolve_rows(o, a, b):
-        top = a - 80
+    def convolve_rows(o, a, b, first, last, lead=0):
+        base = a - 48
+        top = lead or first - 32
         for s in range(16):
-            zp[top:b, s * 128 : (s + 1) * 128] = zst[o, pl.ds(top - s, b - top), :].astype(BF16)
-        total = dot_t(zp[a - 48 : b, :], wat[0])
-        total = total + dot_t(zp[a - 64 : b - 16, :], wat[1])
-        acc[0 : b - a + 48] = total + dot_t(zp[a - 80 : b - 32, :], wat[2])
+            lanes = slice(s * 128, (s + 1) * 128)
+            zp[top:last, lanes] = zst[o, pl.ds(top - s, last - top), :].astype(BF16)
+        total = dot_t(zp[first:last, :], wat[0])
+        total = total + dot_t(zp[first - 16 : last - 16, :], wat[1])
+        acc[first - base : last - base] = total + dot_t(zp[first - 32 : last - 32, :], wat[2])
 
     def residual_rows(a, b):
         n = b - a + 48
@@ -250,7 +254,7 @@
         value = sgx[a:b].astype(F32) - made
         rst[a:b] = jnp.where(in_window(a, b) < segments * SEG, value, 0.0)
 
-    def update_rows(o, step, a, b):
+    def update_rows(o, step, a, b, following):
         n, i = b - a, o * INNER + step
         half = n // 2
         end = b + 80
@@ -297,6 +301,11 @@
             stepped = zst[o, a + low : a + high] + code_rate * scores
             value = stepped - jnp.clip(stepped, -limit, limit)
             zst[o, a + low : a + high] = jnp.where(in_window(a + low, a + high) >= 0, value, 0.0)
+            middle, (c, d) = a + half, following
+            if part == 0:
+                convolve_rows(o, c, d, c - 48, middle)
+            else:
+                convolve_rows(o, c, d, middle, d, middle)
 
     def lanes_sum(row):
         total = row[:, 0:128] + row[:, 128:256] + row[:, 256:384]
@@ -510,7 +519,7 @@
             for copy in halo_copies(1):
                 copy.wait()
             clear_early(1)
-            convolve_rows(1, 96, 608)
+            convolve_rows(1, 96, 608, 48, 608)
             for half in range(2):
                 block_codes[16:ROWS, half * 128 : half * 128 + 128] = dot(
                     zp[16:ROWS, half * 1024 : half * 1024 + 1024], pick[0]
@@ -524,14 +533,13 @@
 
     block_low[:, CHANS:128] = jnp.zeros((2, 128 - CHANS, 1536), BF16)
     clear_early(0)
-    convolve_rows(0, 96, 608)
+    convolve_rows(0, 96, 608, 48, 608)
 
     def outer(o, carry):
         residual_rows(96, 608)
-        update_rows(o, 0, 96, 512)
-        convolve_rows(o, 192, 512)
+        update_rows(o, 0, 96, 512, (192, 512))
         residual_rows(192, 512)
-        update_rows(o, 1, 192, 416)
+        update_rows(o, 1, 192, 416, (288, 416))
 
         @pl.when(o < OUTER - 1)
         def _():
@@ -540,7 +548,6 @@
             for copy in halo_copies(1):
                 copy.start()
 
-        convolve_rows(o, 288, 416)
         residual_rows(288, 416)
         renew(o)
 
@@ -552,6 +559,10 @@
         return carry
 
     lax.fori_loop(0, OUTER, outer, 0)
+    atom_block = lax.broadcasted_iota(jnp.int32, (K, 128), 0) // BLOCK_ATOMS
+    owner_out[...] = jnp.where(atom_block == plan_ref[0], 1, 0) + jnp.where(
+        atom_block == plan_ref[1], 2, 0
+    )
     codes_out[...] = zst[OUTER - 1, OWN : OWN + SEG].T
     write_rows(OUTER - 1)
 
@@ -561,16 +572,17 @@
     depth = segments // PLANE
     vmem = pl.BlockSpec(memory_space=pltpu.VMEM)
     dma = pltpu.SemaphoreType.DMA
-    codes, resid, *rows = pl.pallas_call(
+    codes, resid, first, last, owner = pl.pallas_call(
         functools.partial(kernel, segments),
         out_shape=(
             jax.ShapeDtypeStruct((K, SEG), F32),
             jax.ShapeDtypeStruct((CHANS, SEG), F32),
         )
-        + (jax.ShapeDtypeStruct((BLOCK_ATOMS, CHANS * L), F32),) * OUTER,
+        + (jax.ShapeDtypeStruct((BLOCK_ATOMS, CHANS * L), F32),) * OUTER
+        + (jax.ShapeDtypeStruct((K, 128), jnp.int32),),
         in_specs=[pl.BlockSpec(memory_space=pltpu.SMEM), pl.BlockSpec(memory_space=pl.ANY)]
         + [vmem] * 3,
-        out_specs=(vmem,) * 4,
+        out_specs=(vmem,) * 5,
         scratch_shapes=[
             pltpu.VMEM((OUTER, ROWS, 128), F32),
             pltpu.VMEM((OUTER, SEG, 128), F32),
@@ -619,14 +631,13 @@
             dma,
         ],
         compiler_params=pltpu.CompilerParams(
-            collective_id=0, has_side_effects=True, vmem_limit_bytes=60 * 1024 * 1024
+            collective_id=0, has_side_effects=True, vmem_limit_bytes=VMEM_LIMIT
         ),
     )(plan, turned, codes_init, signal, threshold[None, :])
-    dictionary = dictionary_init.reshape(K // BLOCK_ATOMS, BLOCK_ATOMS, CHANS * L)
-    block = jnp.arange(K // BLOCK_ATOMS)[:, None, None]
-    for o in range(OUTER):
-        dictionary = jnp.where(block == plan[o], rows[o], dictionary)
-    return codes, dictionary.reshape(K, CHANS * L), resid
+    owner = owner[:, :1]
+    first, last = (jnp.tile(rows, (K // BLOCK_ATOMS, 1)) for rows in (first, last))
+    dictionary = jnp.where(owner == 1, first, jnp.where(owner == 2, last, dictionary_init))
+    return codes, dictionary, resid
 
 
 def solution(mesh):

time: 130 us -> 130 us (level)
  Pallas kernels: 113 us -> 117 us
  other arithmetic: 6.93 us -> 3.06 us
    pallas_call x1, Pallas kernels: 113 us -> 117 us  [shards(): pl.pallas_call(functools.partial(kernel, segments), out_shape=(jax.ShapeD...]
    select_n x1, other arithmetic: 5.63 us -> 2.96 us  [shards(): jnp.where(owner == 1, first, jnp.where(owner == 2, last, dictionary_init))]
    unnamed x7 -> x15, local copies, waits for them, and re-layouts: 7.3 us -> 9.67 us
    slice x1 -> x0, local copies, waits for them, and re-layouts: 1.31 us -> none  [shards(): dictionary = jnp.where(block == plan[o], rows[o], dictionary)]
where the time goes in v3:
time: 130 us
  Pallas kernels  117 us (90%)
  local copies, waits for them, and re-layouts  9.67 us (7%)
  other arithmetic  3.06 us (2%)
    pallas_call x1, Pallas kernels, shards(): pl.pallas_call(functools.partial(kernel, segments), out_shape=(jax.ShapeD...  117 us
    unnamed x15, local copies, waits for them, and re-layouts  9.67 us
    select_n x1, other arithmetic, shards(): jnp.where(owner == 1, first, jnp.where(owner == 2, last, dictionary_init))  2.96 us

profile of v3, /device:TPU:1, one launch (start us, length us, event | category | flops | bytes accessed | tf_op | source)
XLA Modules:
  0.0 130.1 jit_solution(4955590712941007213)
XLA Ops:
  0.6 0.0 copy-start.1
  0.6 0.0 copy-start.2
  0.7 0.0 copy-start.3
  0.7 0.0 copy-start.4
  0.7 6.1 %copy.9 = f32[128,9216]{0,1:T(8,128)} copy(f32[128,9216]{1,0:T(8,128)} %param.7) | data formatting | bytes 9437184 | tf_op args[2]
  6.7 0.0 copy-done.1
  6.7 0.0 copy-done.2
  6.7 0.0 copy-done.3
  6.8 0.0 copy-done.4
  6.8 0.0 copy-start
  6.8 2.3 %copy-done = f32[128,9216]{0,1:T(8,128)S(1)} copy-done((f32[128,9216]{0,1:T(8,128)S(1)}, f32[128,9216]{0,1:T(8,128)}, u32[]{:S(2)}) %copy-start) | copy-done | bytes 4718616
  9.1 0.0 copy-start.5
  9.1 116.7 %shard_map.76 = (f32[128,128]{1,0:T(8,128)S(1)}, f32[96,128]{1,0:T(8,128)S(1)}, f32[16,9216]{1,0:T(8,128)S(1)}, f32[16,9216]{1,0:T(8,128)S(1)}, s32[128,128]{1,0:T(8,128)S(1)}) custom-call(s32[8]{0:T(128)S(1)} %copy-done.3, f32[9216,128]{1,0:T(8,128)S(1)} %bitcast.8, f32[128,128]{1,0:T(8,128)S(1)} %copy-done.1, bf16[96,128]{1,0:T(8,128)(2,1)S(1)} %copy-done.2, ...), custom_call_target="tpu_custom_call" | custom-call | tf_op jit(solution)/shard_map/pallas_call | solution.py:575
  125.8 0.1 compare_reduce_fusion.1
  125.9 0.0 copy-done.5
  125.9 3.0 %fusion = f32[128,9216]{1,0:T(8,128)} fusion(f32[128,9216]{1,0:T(8,128)S(1)} %copy-done.5, f32[16,9216]{1,0:T(8,128)S(1)} %get-tuple-element.11, f32[16,9216]{1,0:T(8,128)S(1)} %get-tuple-element.10, pred[128]{0:T(512)(128)(4,1)S(1)} %get-tuple-element.14, pred[128]{0:T(512)(128)(4,1)S(1)} %get-tuple-element.13), kind=kLoop, calls=%fused_computation.1 | loop fusion | flops 2359296 | bytes 10617088 | tf_op jit(solution)/shard_map/jit(_where)/select_n | solution.py:639
  128.9 0.6 copy.12
  129.5 0.6 copy.13
Async XLA Ops:
  0.6 6.1 %copy-start.1 = (f32[128,128]{1,0:T(8,128)S(1)}, f32[128,128]{1,0:T(8,128)}, u32[]{:S(2)}) copy-start(f32[128,128]{1,0:T(8,128)} %codes_ref.1) | copy-start | bytes 196612
  0.6 6.1 %copy-start.2 = (bf16[96,128]{1,0:T(8,128)(2,1)S(1)}, bf16[96,128]{1,0:T(8,128)(2,1)}, u32[]{:S(2)}) copy-start(bf16[96,128]{1,0:T(8,128)(2,1)} %signal_ref.1) | copy-start | bytes 73732
  0.7 6.1 %copy-start.3 = (s32[8]{0:T(128)S(1)}, s32[8]{0:T(128)}, u32[]{:S(2)}) copy-start(s32[8]{0:T(128)} %plan_ref.1) | copy-start | bytes 100
  0.7 6.1 %copy-start.4 = (f32[128]{0:T(128)S(1)}, f32[128]{0:T(128)}, u32[]{:S(2)}) copy-start(f32[128]{0:T(128)} %param.8) | copy-start | bytes 1540
  6.8 2.3 %copy-start = (f32[128,9216]{0,1:T(8,128)S(1)}, f32[128,9216]{0,1:T(8,128)}, u32[]{:S(2)}) copy-start(f32[128,9216]{0,1:T(8,128)} %copy.9) | copy-start | bytes 14155780
  9.1 116.8 %copy-start.5 = (f32[128,9216]{1,0:T(8,128)S(1)}, f32[128,9216]{1,0:T(8,128)}, u32[]{:S(2)}) copy-start(f32[128,9216]{1,0:T(8,128)} %param.7) | copy-start | bytes 14155780

commit v4 on v2

--- a/solution.py
+++ b/solution.py
@@ -21,6 +21,7 @@
 move_rate = 0.5
 tiny_eps = 1e-06
 
+VMEM_LIMIT = 32 * 1024 * 1024
 MESH = pl.DeviceIdType.MESH
 F32 = jnp.float32
 BF16 = jnp.bfloat16
@@ -54,7 +55,7 @@
 def kernel(
     segments,
     plan_ref,
-    dt_hbm,
+    dict_ref,
     codes_ref,
     signal_ref,
     thr_ref,
@@ -62,6 +63,7 @@
     resid_out,
     rows_first,
     rows_last,
+    owner_out,
     zst,
     zsend,
     sgx,
@@ -106,7 +108,6 @@
     a_recv,
     t_send,
     t_recv,
-    load_sem,
 ):
     unit = ENTRIES ** (-0.5)
     tm = lax.axis_index("tm")
@@ -127,8 +128,6 @@
     partner = chan + 1 - 2 * (chan % 2)
     opposite = (chan + 2) % 4
 
-    load = pltpu.make_async_copy(dt_hbm, dt_ref, load_sem)
-    load.start()
     zsend[0] = codes_ref[...].T
     zst[0, OWN : OWN + SEG] = zsend[0]
     low = jnp.concatenate(
@@ -138,6 +137,13 @@
     sgx[OWN : OWN + SEG] = low
 
 
+    barrier = pltpu.get_barrier_semaphore()
+    peers = [{"tm": seg(d)} for d in (-3, -2, -1, 1, 2, 3)]
+    peers += [{"chan": (chan + d) % 4} for d in range(1, 4)]
+    peers += [{"tm": in_plane(d)} for d in range(1, PLANE)]
+    peers += [{"tm": in_depth(d)} for d in range(1, depth)]
+    for peer in peers:
+        pl.semaphore_signal(barrier, inc=1, device_id=peer, device_id_type=MESH)
     def pick_body(o, carry):
         tall = lax.broadcasted_iota(jnp.int32, (1024, 128), 0)
         wide = lax.broadcasted_iota(jnp.int32, (1024, 128), 1)
@@ -150,13 +156,13 @@
 
     lax.fori_loop(0, OUTER, pick_body, 0)
 
-    barrier = pltpu.get_barrier_semaphore()
-    peers = [{"tm": seg(d)} for d in (-3, -2, -1, 1, 2, 3)]
-    peers += [{"chan": (chan + d) % 4} for d in range(1, 4)]
-    peers += [{"tm": in_plane(d)} for d in range(1, PLANE)]
-    peers += [{"tm": in_depth(d)} for d in range(1, depth)]
-    for peer in peers:
-        pl.semaphore_signal(barrier, inc=1, device_id=peer, device_id_type=MESH)
+    for m in range(CHANS // 4):
+        tiles = [dict_ref[:, m * 384 + t * 128 : m * 384 + t * 128 + 128].T for t in range(3)]
+        turned = jnp.concatenate(tiles, axis=0)
+        for r in range(4):
+            row = (4 * m + r) * 97
+            dt_ref[row : row + L] = turned[r * L : (r + 1) * L]
+
     pl.semaphore_wait(barrier, len(peers))
 
     def remote(src, dst, send, recv, peer):
@@ -200,7 +206,6 @@
             wb[q, s * 128 + CHANS : (s + 1) * 128] = jnp.zeros((128 - CHANS, 256), BF16)
         for j in range(2):
             wat[q, j * 128 + CHANS : (j + 1) * 128] = jnp.zeros((128 - CHANS, 2048), BF16)
-    load.wait()
     lane_block = lax.broadcasted_iota(jnp.int32, (CHANS, 128), 1) // BLOCK_ATOMS
 
     def arrange(i, carry):
@@ -210,7 +215,7 @@
             found = [jnp.zeros((CHANS, 128), F32)] * OUTER
             for k in range(8):
                 s = half * 8 + k
-                value = dt_ref[pl.ds(16 * i + s, CHANS, stride=L), :]
+                value = dt_ref[pl.ds(16 * i + s, CHANS, stride=97), :]
                 low = value.astype(BF16)
                 wb[q, s * 128 : s * 128 + CHANS, pl.ds(here, 128)] = low
                 wat[q, pl.ds(here, CHANS), s * 128 : (s + 1) * 128] = low
@@ -552,25 +557,28 @@
         return carry
 
     lax.fori_loop(0, OUTER, outer, 0)
+    atom_block = lax.broadcasted_iota(jnp.int32, (K, 128), 0) // BLOCK_ATOMS
+    owner_out[...] = jnp.where(atom_block == plan_ref[0], 1, 0) + jnp.where(
+        atom_block == plan_ref[1], 2, 0
+    )
     codes_out[...] = zst[OUTER - 1, OWN : OWN + SEG].T
     write_rows(OUTER - 1)
 
 
 def shards(segments, signal, codes_init, dictionary_init, threshold, plan):
-    turned = dictionary_init.T
     depth = segments // PLANE
     vmem = pl.BlockSpec(memory_space=pltpu.VMEM)
     dma = pltpu.SemaphoreType.DMA
-    codes, resid, *rows = pl.pallas_call(
+    codes, resid, first, last, owner = pl.pallas_call(
         functools.partial(kernel, segments),
         out_shape=(
             jax.ShapeDtypeStruct((K, SEG), F32),
             jax.ShapeDtypeStruct((CHANS, SEG), F32),
         )
-        + (jax.ShapeDtypeStruct((BLOCK_ATOMS, CHANS * L), F32),) * OUTER,
-        in_specs=[pl.BlockSpec(memory_space=pltpu.SMEM), pl.BlockSpec(memory_space=pl.ANY)]
-        + [vmem] * 3,
-        out_specs=(vmem,) * 4,
+        + (jax.ShapeDtypeStruct((BLOCK_ATOMS, CHANS * L), F32),) * OUTER
+        + (jax.ShapeDtypeStruct((K, 128), jnp.int32),),
+        in_specs=[pl.BlockSpec(memory_space=pltpu.SMEM)] + [vmem] * 4,
+        out_specs=(vmem,) * 5,
         scratch_shapes=[
             pltpu.VMEM((OUTER, ROWS, 128), F32),
             pltpu.VMEM((OUTER, SEG, 128), F32),
@@ -595,7 +603,7 @@
             pltpu.VMEM((OUTER, CHANS, 1536), F32),
             pltpu.VMEM((OUTER, CHANS, 1536), F32),
             pltpu.VMEM((OUTER, 1024, 128), BF16),
-            pltpu.VMEM((CHANS * L, K), F32),
+            pltpu.VMEM((CHANS * 97, K), F32),
             pltpu.VMEM((ROWS, 256), BF16),
             pltpu.VMEM((2, 128, 1536), BF16),
             pltpu.VMEM((1536, 128), F32),
@@ -616,17 +624,15 @@
             dma((OUTER, PLANE, 3)),
             dma((OUTER, 4)),
             dma((OUTER, 4)),
-            dma,
         ],
         compiler_params=pltpu.CompilerParams(
-            collective_id=0, has_side_effects=True, vmem_limit_bytes=60 * 1024 * 1024
+            collective_id=0, has_side_effects=True, vmem_limit_bytes=VMEM_LIMIT
         ),
-    )(plan, turned, codes_init, signal, threshold[None, :])
-    dictionary = dictionary_init.reshape(K // BLOCK_ATOMS, BLOCK_ATOMS, CHANS * L)
-    block = jnp.arange(K // BLOCK_ATOMS)[:, None, None]
-    for o in range(OUTER):
-        dictionary = jnp.where(block == plan[o], rows[o], dictionary)
-    return codes, dictionary.reshape(K, CHANS * L), resid
+    )(plan, dictionary_init, codes_init, signal, threshold[None, :])
+    owner = owner[:, :1]
+    first, last = (jnp.tile(rows, (K // BLOCK_ATOMS, 1)) for rows in (first, last))
+    dictionary = jnp.where(owner == 1, first, jnp.where(owner == 2, last, dictionary_init))
+    return codes, dictionary, resid
 
 
 def solution(mesh):

time: 130 us -> 122 us (0.938)
  other arithmetic: 6.93 us -> 3.14 us
  local copies, waits for them, and re-layouts: 8.94 us -> 6.46 us
  Pallas kernels: 113 us -> 111 us
    select_n x1, other arithmetic: 5.63 us -> 3.04 us  [shards(): jnp.where(owner == 1, first, jnp.where(owner == 2, last, dictionary_init))]
    pallas_call x1, Pallas kernels: 113 us -> 111 us  [shards(): pl.pallas_call(functools.partial(kernel, segments), out_shape=(jax.ShapeD...]
    slice x1 -> x0, local copies, waits for them, and re-layouts: 1.31 us -> none  [shards(): dictionary = jnp.where(block == plan[o], rows[o], dictionary)]
    unnamed x7 -> x12, local copies, waits for them, and re-layouts: 7.3 us -> 6.46 us
where the time goes in v4:
time: 122 us; the launch traced here: 121 us
  Pallas kernels  111 us (91%)
  local copies, waits for them, and re-layouts  6.46 us (5%)
  other arithmetic  3.14 us (3%)
    pallas_call x1, Pallas kernels, shards(): pl.pallas_call(functools.partial(kernel, segments), out_shape=(jax.ShapeD...  111 us
    unnamed x12, local copies, waits for them, and re-layouts  6.46 us
    select_n x1, other arithmetic, shards(): jnp.where(owner == 1, first, jnp.where(owner == 2, last, dictionary_init))  3.04 us

profile of v4, /device:TPU:1, one launch (start us, length us, event | category | flops | bytes accessed | tf_op | source)
XLA Modules:
  0.0 121.3 jit_solution(7461361787056376094)
XLA Ops:
  0.6 0.0 copy-start
  0.6 2.3 %copy-done = f32[128,9216]{1,0:T(8,128)S(1)} copy-done((f32[128,9216]{1,0:T(8,128)S(1)}, f32[128,9216]{1,0:T(8,128)}, u32[]{:S(2)}) %copy-start) | copy-done | bytes 4718616
  3.0 0.0 copy-start.1
  3.0 0.8 copy-done.1
  3.8 0.0 copy-start.2
  3.8 0.7 copy-done.2
  4.5 0.0 copy-start.3
  4.5 0.7 copy-done.3
  5.2 0.0 copy-start.4
  5.2 0.7 copy-done.4
  5.9 111.0 %shard_map.76 = (f32[128,128]{1,0:T(8,128)S(1)}, f32[96,128]{1,0:T(8,128)S(1)}, f32[16,9216]{1,0:T(8,128)S(1)}, f32[16,9216]{1,0:T(8,128)S(1)}, s32[128,128]{1,0:T(8,128)S(1)}) custom-call(s32[8]{0:T(128)S(1)} %copy-done.3, f32[128,9216]{1,0:T(8,128)S(1)} %copy-done, f32[128,128]{1,0:T(8,128)S(1)} %copy-done.1, bf16[96,128]{1,0:T(8,128)(2,1)S(1)} %copy-done.2, ...), custom_call_target="tpu_custom_call" | custom-call | tf_op jit(solution)/shard_map/pallas_call | solution.py:572
  116.9 0.1 compare_reduce_fusion.1
  117.0 3.0 %fusion = f32[128,9216]{1,0:T(8,128)} fusion(f32[128,9216]{1,0:T(8,128)S(1)} %copy-done, f32[16,9216]{1,0:T(8,128)S(1)} %get-tuple-element.11, f32[16,9216]{1,0:T(8,128)S(1)} %get-tuple-element.10, pred[128]{0:T(512)(128)(4,1)S(1)} %get-tuple-element.14, pred[128]{0:T(512)(128)(4,1)S(1)} %get-tuple-element.13), kind=kLoop, calls=%fused_computation.1 | loop fusion | flops 2359296 | bytes 10617088 | tf_op jit(solution)/shard_map/jit(_where)/select_n | solution.py:634
  120.1 0.6 copy.10
  120.7 0.6 copy.11
Async XLA Ops:
  0.6 2.3 %copy-start = (f32[128,9216]{1,0:T(8,128)S(1)}, f32[128,9216]{1,0:T(8,128)}, u32[]{:S(2)}) copy-start(f32[128,9216]{1,0:T(8,128)} %dict_ref.1) | copy-start | bytes 14155780
  3.0 0.8 copy-start.1
  3.8 0.7 copy-start.2
  4.5 0.7 copy-start.3
  5.2 0.7 copy-start.4

commit v5 on v4

--- a/solution.py
+++ b/solution.py
@@ -56,9 +56,7 @@
     segments,
     plan_ref,
     dict_ref,
-    codes_ref,
-    signal_ref,
-    thr_ref,
+    small_ref,
     codes_out,
     resid_out,
     rows_first,
@@ -94,6 +92,7 @@
     in_order,
     by_atom,
     strecv,
+    plane_sums,
     h_send,
     h_recv,
     s_send,
@@ -108,6 +107,8 @@
     a_recv,
     t_send,
     t_recv,
+    u_send,
+    u_recv,
 ):
     unit = ENTRIES ** (-0.5)
     tm = lax.axis_index("tm")
@@ -128,10 +129,10 @@
     partner = chan + 1 - 2 * (chan % 2)
     opposite = (chan + 2) % 4
 
-    zsend[0] = codes_ref[...].T
+    zsend[0] = small_ref[0:K].T
     zst[0, OWN : OWN + SEG] = zsend[0]
     low = jnp.concatenate(
-        [signal_ref[...].astype(F32), jnp.zeros((SEG - CHANS, SEG), F32)], axis=0
+        [small_ref[K : K + CHANS], jnp.zeros((SEG - CHANS, SEG), F32)], axis=0
     ).T.astype(BF16)
     sgown[...] = low
     sgx[OWN : OWN + SEG] = low
@@ -294,7 +295,7 @@
             )
             copy.start()
             far.append(copy)
-        limit = thr_ref[...]
+        limit = small_ref[K + CHANS : K + CHANS + 1]
         for part in range(2):
             low, high = part * half, (part + 1) * half
             far[part].wait()
@@ -313,6 +314,28 @@
     def old_piece(o, piece):
         top, left = piece // 4 * 48, piece % 4 * 384
         return old[o, top : top + 48, left : left + 384]
+
+    def coef_of(with_old, old_old):
+        return jnp.where(old_old > 0.0, with_old / jnp.maximum(old_old, 1e-30), 0.0)
+
+    def packed(with_old, old_old, left_over):
+        row = lax.broadcasted_iota(jnp.int32, (8, 128), 0)
+        return jnp.where(row == 0, with_old, jnp.where(row == 1, old_old, left_over))
+
+    def total_of(parts, row):
+        total = parts[0][row : row + 1]
+        for part in parts[1:]:
+            total = total + part[row : row + 1]
+        return total
+
+    def pooled(parts, coef):
+        total = jnp.zeros((1, 128), F32)
+        for part in parts:
+            gd, dd, rr = part[0:1], part[1:2], part[2:3]
+            mine = coef_of(gd, dd)
+            off = mine - coef
+            total = total + rr + off * (off * dd + 2.0 * (gd - mine * dd))
+        return total
 
     def three(row):
         return jnp.concatenate([row[0:1]] * 3, axis=1)
@@ -388,54 +411,46 @@
             agbuf[o, place, rows] = total.astype(BF16)
             slot = lambda d: agbuf.at[o, place]
             gather.append(spread_rows(part, plane, slot, slot, a_send, a_recv))
+        grad = agbuf[o, place].astype(F32)
+        top = pl.multiple_of(place // 4 * 48, 16)
+        left = pl.multiple_of(place % 4 * 384, 128)
+        was = old[o, pl.ds(top, 48), pl.ds(left, 384)]
+        with_old = lanes_sum(jnp.sum(grad * was, axis=0, keepdims=True))
+        old_old = lanes_sum(jnp.sum(was * was, axis=0, keepdims=True))
+        part = grad - three(coef_of(with_old, old_old)) * was
+        strecv[o, chan] = packed(
+            with_old, old_old, lanes_sum(jnp.sum(part * part, axis=0, keepdims=True))
+        )
+
+        def share(slot, send, recv, peers):
+            copies = [
+                remote(slot, slot, send.at[o, d], recv.at[o, d], peer) for d, peer in peers
+            ]
+            for copy in copies:
+                copy.start()
+            for copy in copies:
+                copy.wait_recv()
+            sent.extend(copies)
+
+        share(
+            strecv.at[o, chan],
+            t_send,
+            t_recv,
+            [(d, {"chan": (chan + d) % 4}) for d in range(1, 4)],
+        )
+        parts = [strecv[o, i] for i in range(4)]
+        with_old, old_old = total_of(parts, 0), total_of(parts, 1)
+        plane_sums[o, place] = packed(
+            with_old, old_old, pooled(parts, coef_of(with_old, old_old))
+        )
+        share(plane_sums.at[o, place], u_send, u_recv, [(d, {"tm": peer}) for d, peer in plane])
+        parts = [plane_sums[o, i] for i in range(PLANE)]
+        mean_sq = total_of(parts, 1)[0:1] / ENTRIES + tiny_eps
+        along = total_of(parts, 0)[0:1] / ENTRIES / mean_sq
+        spread = jnp.maximum(pooled(parts, along), 0.0) / ENTRIES + tiny_eps
         for copies in gather:
             for copy in copies:
                 copy.wait_recv()
-
-        with_old = jnp.zeros((1, 384), F32)
-        old_old = jnp.zeros((1, 384), F32)
-        for piece in range(PLANE):
-            grad, was = agbuf[o, piece].astype(F32), old_piece(o, piece)
-            with_old = with_old + jnp.sum(grad * was, axis=0, keepdims=True)
-            old_old = old_old + jnp.sum(was * was, axis=0, keepdims=True)
-        with_old, old_old = lanes_sum(with_old), lanes_sum(old_old)
-        own_coef = jnp.where(old_old > 0.0, with_old / jnp.maximum(old_old, 1e-30), 0.0)
-        left_over = jnp.zeros((1, 384), F32)
-        coef = three(own_coef)
-        for piece in range(PLANE):
-            part = agbuf[o, piece].astype(F32) - coef * old_piece(o, piece)
-            left_over = left_over + jnp.sum(part * part, axis=0, keepdims=True)
-        left_over = lanes_sum(left_over)
-        row = lax.broadcasted_iota(jnp.int32, (8, 128), 0)
-        packed = jnp.where(row == 0, with_old, jnp.where(row == 1, old_old, left_over))
-        strecv[o, chan] = packed
-        copies = [
-            remote(
-                strecv.at[o, chan],
-                strecv.at[o, chan],
-                t_send.at[o, d],
-                t_recv.at[o, d],
-                {"chan": (chan + d) % 4},
-            )
-            for d in range(1, 4)
-        ]
-        for copy in copies:
-            copy.start()
-        for copy in copies:
-            copy.wait_recv()
-        sent = sent + copies
-        parts = [strecv[o, i] for i in range(4)]
-        gd = [part[0:1] for part in parts]
-        dd = [part[1:2] for part in parts]
-        rr = [part[2:3] for part in parts]
-        mean_sq = (dd[0] + dd[1] + dd[2] + dd[3]) / ENTRIES + tiny_eps
-        along = (gd[0] + gd[1] + gd[2] + gd[3]) / ENTRIES / mean_sq
-        spread = jnp.zeros((1, 128), F32)
-        for i in range(4):
-            mine = jnp.where(dd[i] > 0.0, gd[i] / jnp.maximum(dd[i], 1e-30), 0.0)
-            off = mine - along
-            spread = spread + rr[i] + off * (off * dd[i] + 2.0 * (gd[i] - mine * dd[i]))
-        spread = jnp.maximum(spread, 0.0) / ENTRIES + tiny_eps
         along_row = three(along)
         gain = three(move_rate / jnp.sqrt(spread))
         shrink = three(1.0 / jnp.sqrt(mean_sq + 0.25))
@@ -566,6 +581,8 @@
 
 
 def shards(segments, signal, codes_init, dictionary_init, threshold, plan):
+    limits = jnp.broadcast_to(threshold[None, :], (8, K))
+    small = jnp.concatenate([codes_init, signal.astype(F32), limits], axis=0)
     depth = segments // PLANE
     vmem = pl.BlockSpec(memory_space=pltpu.VMEM)
     dma = pltpu.SemaphoreType.DMA
@@ -577,7 +594,7 @@
         )
         + (jax.ShapeDtypeStruct((BLOCK_ATOMS, CHANS * L), F32),) * OUTER
         + (jax.ShapeDtypeStruct((K, 128), jnp.int32),),
-        in_specs=[pl.BlockSpec(memory_space=pltpu.SMEM)] + [vmem] * 4,
+        in_specs=[pl.BlockSpec(memory_space=pltpu.SMEM)] + [vmem] * 2,
         out_specs=(vmem,) * 5,
         scratch_shapes=[
             pltpu.VMEM((OUTER, ROWS, 128), F32),
@@ -610,6 +627,7 @@
             pltpu.VMEM((1536, 128), F32),
             pltpu.VMEM((16 * 97, 128), F32),
             pltpu.VMEM((OUTER, 4, 8, 128), F32),
+            pltpu.VMEM((OUTER, PLANE, 8, 128), F32),
             dma((OUTER, 5)),
             dma((OUTER, 5)),
             dma((4,)),
@@ -624,11 +642,13 @@
             dma((OUTER, PLANE, 3)),
             dma((OUTER, 4)),
             dma((OUTER, 4)),
+            dma((OUTER, PLANE)),
+            dma((OUTER, PLANE)),
         ],
         compiler_params=pltpu.CompilerParams(
             collective_id=0, has_side_effects=True, vmem_limit_bytes=VMEM_LIMIT
         ),
-    )(plan, dictionary_init, codes_init, signal, threshold[None, :])
+    )(plan, dictionary_init, small)
     owner = owner[:, :1]
     first, last = (jnp.tile(rows, (K // BLOCK_ATOMS, 1)) for rows in (first, last))
     dictionary = jnp.where(owner == 1, first, jnp.where(owner == 2, last, dictionary_init))

time: 122 us -> 121 us (level)
  local copies, waits for them, and re-layouts: 6.46 us -> 4.89 us
  other arithmetic: 3.14 us -> 4.67 us
    unnamed x12 -> x6, local copies, waits for them, and re-layouts: 6.46 us -> 4.23 us
where the time goes in v5:
time: 121 us
  Pallas kernels  111 us (92%)
  local copies, waits for them, and re-layouts  4.89 us (4%)
  other arithmetic  4.67 us (4%)
    pallas_call x1, Pallas kernels, shards(): pl.pallas_call(functools.partial(kernel, segments), out_shape=(jax.ShapeD...  111 us
    unnamed x6, local copies, waits for them, and re-layouts  4.23 us
    select_n x1, other arithmetic, shards(): jnp.where(owner == 1, first, jnp.where(owner == 2, last, dictionary_init))  2.97 us

profile of v5, /device:TPU:1, one launch (start us, length us, event | category | flops | bytes accessed | tf_op | source)
XLA Modules:
  0.0 121.2 jit_solution(14251953958847969317)
XLA Ops:
  0.6 0.7 broadcast_in_dim.23
  1.3 0.7 convert_element_type.3
  2.0 0.8 pad_maximum_fusion.small_ref
  2.9 0.0 copy-start
  2.9 2.3 %copy-done = f32[128,9216]{1,0:T(8,128)S(1)} copy-done((f32[128,9216]{1,0:T(8,128)S(1)}, f32[128,9216]{1,0:T(8,128)}, u32[]{:S(2)}) %copy-start) | copy-done | bytes 4718616
  5.2 0.0 copy-start.1
  5.2 0.7 copy-done.1
  5.9 111.0 %shard_map.76 = (f32[128,128]{1,0:T(8,128)S(1)}, f32[96,128]{1,0:T(8,128)S(1)}, f32[16,9216]{1,0:T(8,128)S(1)}, f32[16,9216]{1,0:T(8,128)S(1)}, s32[128,128]{1,0:T(8,128)S(1)}) custom-call(s32[8]{0:T(128)S(1)} %copy-done.1, f32[128,9216]{1,0:T(8,128)S(1)} %copy-done, f32[232,128]{1,0:T(8,128)S(1)} %pad_maximum_fusion.small_ref), custom_call_target="tpu_custom_call" | custom-call | tf_op jit(solution)/shard_map/pallas_call | solution.py:589
  116.9 0.1 compare_reduce_fusion.1
  117.0 3.0 %fusion = f32[128,9216]{1,0:T(8,128)} fusion(f32[128,9216]{1,0:T(8,128)S(1)} %copy-done, f32[16,9216]{1,0:T(8,128)S(1)} %get-tuple-element.11, f32[16,9216]{1,0:T(8,128)S(1)} %get-tuple-element.10, pred[128]{0:T(512)(128)(4,1)S(1)} %get-tuple-element.14, pred[128]{0:T(512)(128)(4,1)S(1)} %get-tuple-element.13), kind=kLoop, calls=%fused_computation.1 | loop fusion | flops 2359296 | bytes 10617088 | tf_op jit(solution)/shard_map/jit(_where)/select_n | solution.py:654
  119.9 0.6 copy.10
  120.6 0.6 copy.11
Async XLA Ops:
  2.9 2.3 %copy-start = (f32[128,9216]{1,0:T(8,128)S(1)}, f32[128,9216]{1,0:T(8,128)}, u32[]{:S(2)}) copy-start(f32[128,9216]{1,0:T(8,128)} %dict_ref.1) | copy-start | bytes 14155780
  5.2 0.7 copy-start.1

commit v6 on v5

--- a/solution.py
+++ b/solution.py
@@ -22,6 +22,7 @@
 tiny_eps = 1e-06
 
 VMEM_LIMIT = 32 * 1024 * 1024
+PARTS = 9
 MESH = pl.DeviceIdType.MESH
 F32 = jnp.float32
 BF16 = jnp.bfloat16
@@ -359,12 +360,15 @@
             gsend[piece] = gfull[top : top + 48, left : left + 384]
         sent = []
 
+        def part_of(part):
+            return pl.ds(part % 3 * 16, 16), pl.ds(part // 3 * 128, 128)
+
         def spread_rows(part, peers, source, target, send, recv):
-            rows = pl.ds(part * 16, 16)
+            rows, lanes = part_of(part)
             copies = [
                 remote(
-                    source(d).at[rows],
-                    target(d).at[rows],
+                    source(d).at[rows, lanes],
+                    target(d).at[rows, lanes],
                     send.at[o, d, part],
                     recv.at[o, d, part],
                     {"tm": peer},
@@ -387,28 +391,28 @@
                 p_send,
                 p_recv,
             )
-            for part in range(3)
+            for part in range(PARTS)
         ]
         cover(o)
         across_levels = []
-        for part in range(3):
-            rows = pl.ds(part * 16, 16)
-            total = gsend[place, rows].astype(F32)
+        for part in range(PARTS):
+            rows, lanes = part_of(part)
+            total = gsend[place, rows, lanes].astype(F32)
             for d, copy in enumerate(scatter[part], 1):
                 copy.wait_recv()
-                total = total + grecv[o, d, rows].astype(F32)
-            zbuf[o, level, rows] = total.astype(BF16)
+                total = total + grecv[o, d, rows, lanes].astype(F32)
+            zbuf[o, level, rows, lanes] = total.astype(BF16)
             slot = lambda d: zbuf.at[o, level]
             across_levels.append(spread_rows(part, levels, slot, slot, z_send, z_recv))
         gather = []
-        for part in range(3):
-            rows = pl.ds(part * 16, 16)
+        for part in range(PARTS):
+            rows, lanes = part_of(part)
             for copy in across_levels[part]:
                 copy.wait_recv()
-            total = zbuf[o, 0, rows].astype(F32)
+            total = zbuf[o, 0, rows, lanes].astype(F32)
             for i in range(1, depth):
-                total = total + zbuf[o, i, rows].astype(F32)
-            agbuf[o, place, rows] = total.astype(BF16)
+                total = total + zbuf[o, i, rows, lanes].astype(F32)
+            agbuf[o, place, rows, lanes] = total.astype(BF16)
             slot = lambda d: agbuf.at[o, place]
             gather.append(spread_rows(part, plane, slot, slot, a_send, a_recv))
         grad = agbuf[o, place].astype(F32)
@@ -634,12 +638,12 @@
             dma((4,)),
             dma((4, 2, 2)),
             dma((4, 2, 2)),
-            dma((OUTER, PLANE, 3)),
-            dma((OUTER, PLANE, 3)),
-            dma((OUTER, depth, 3)),
-            dma((OUTER, depth, 3)),
-            dma((OUTER, PLANE, 3)),
-            dma((OUTER, PLANE, 3)),
+            dma((OUTER, PLANE, PARTS)),
+            dma((OUTER, PLANE, PARTS)),
+            dma((OUTER, depth, PARTS)),
+            dma((OUTER, depth, PARTS)),
+            dma((OUTER, PLANE, PARTS)),
+            dma((OUTER, PLANE, PARTS)),
             dma((OUTER, 4)),
             dma((OUTER, 4)),
             dma((OUTER, PLANE)),

time: 121 us -> 127 us (1.050)
  Pallas kernels: 111 us -> 117 us
    pallas_call x1, Pallas kernels: 111 us -> 117 us  [shards(): pl.pallas_call(functools.partial(kernel, segments), out_shape=(jax.ShapeD...]
where the time goes in v6:
time: 127 us
  Pallas kernels  117 us (92%)
  local copies, waits for them, and re-layouts  4.89 us (4%)
  other arithmetic  4.67 us (4%)
    pallas_call x1, Pallas kernels, shards(): pl.pallas_call(functools.partial(kernel, segments), out_shape=(jax.ShapeD...  117 us
    unnamed x6, local copies, waits for them, and re-layouts  4.23 us
    select_n x1, other arithmetic, shards(): jnp.where(owner == 1, first, jnp.where(owner == 2, last, dictionary_init))  2.97 us

profile of v6, /device:TPU:1, one launch (start us, length us, event | category | flops | bytes accessed | tf_op | source)
XLA Modules:
  0.0 126.9 jit_solution(3746691985362999688)
XLA Ops:
  0.6 0.7 broadcast_in_dim.23
  1.3 0.7 convert_element_type.3
  2.0 0.8 pad_maximum_fusion.small_ref
  2.9 0.0 copy-start
  2.9 2.3 %copy-done = f32[128,9216]{1,0:T(8,128)S(1)} copy-done((f32[128,9216]{1,0:T(8,128)S(1)}, f32[128,9216]{1,0:T(8,128)}, u32[]{:S(2)}) %copy-start) | copy-done | bytes 4718616
  5.2 0.0 copy-start.1
  5.2 0.7 copy-done.1
  5.9 116.7 %shard_map.76 = (f32[128,128]{1,0:T(8,128)S(1)}, f32[96,128]{1,0:T(8,128)S(1)}, f32[16,9216]{1,0:T(8,128)S(1)}, f32[16,9216]{1,0:T(8,128)S(1)}, s32[128,128]{1,0:T(8,128)S(1)}) custom-call(s32[8]{0:T(128)S(1)} %copy-done.1, f32[128,9216]{1,0:T(8,128)S(1)} %copy-done, f32[232,128]{1,0:T(8,128)S(1)} %pad_maximum_fusion.small_ref), custom_call_target="tpu_custom_call" | custom-call | tf_op jit(solution)/shard_map/pallas_call | solution.py:593
  122.6 0.1 compare_reduce_fusion.1
  122.7 3.0 %fusion = f32[128,9216]{1,0:T(8,128)} fusion(f32[128,9216]{1,0:T(8,128)S(1)} %copy-done, f32[16,9216]{1,0:T(8,128)S(1)} %get-tuple-element.11, f32[16,9216]{1,0:T(8,128)S(1)} %get-tuple-element.10, pred[128]{0:T(512)(128)(4,1)S(1)} %get-tuple-element.14, pred[128]{0:T(512)(128)(4,1)S(1)} %get-tuple-element.13), kind=kLoop, calls=%fused_computation.1 | loop fusion | flops 2359296 | bytes 10617088 | tf_op jit(solution)/shard_map/jit(_where)/select_n | solution.py:658
  125.7 0.6 copy.10
  126.3 0.6 copy.11
Async XLA Ops:
  2.9 2.3 %copy-start = (f32[128,9216]{1,0:T(8,128)S(1)}, f32[128,9216]{1,0:T(8,128)}, u32[]{:S(2)}) copy-start(f32[128,9216]{1,0:T(8,128)} %dict_ref.1) | copy-start | bytes 14155780
  5.2 0.7 copy-start.1

commit v7 on v6

--- a/solution.py
+++ b/solution.py
@@ -22,7 +22,7 @@
 tiny_eps = 1e-06
 
 VMEM_LIMIT = 32 * 1024 * 1024
-PARTS = 9
+PARTS = 3
 MESH = pl.DeviceIdType.MESH
 F32 = jnp.float32
 BF16 = jnp.bfloat16
@@ -361,7 +361,7 @@
         sent = []
 
         def part_of(part):
-            return pl.ds(part % 3 * 16, 16), pl.ds(part // 3 * 128, 128)
+            return pl.ds(part * 16, 16), pl.ds(0, 384)
 
         def spread_rows(part, peers, source, target, send, recv):
             rows, lanes = part_of(part)
@@ -404,6 +404,34 @@
             zbuf[o, level, rows, lanes] = total.astype(BF16)
             slot = lambda d: zbuf.at[o, level]
             across_levels.append(spread_rows(part, levels, slot, slot, z_send, z_recv))
+
+        def share(slot, send, recv, peers):
+            copies = [
+                remote(slot, slot, send.at[o, d], recv.at[o, d], peer) for d, peer in peers
+            ]
+            for copy in copies:
+                copy.start()
+            sent.extend(copies)
+            return copies
+
+        def sums_over_chan():
+            grad = agbuf[o, place].astype(F32)
+            top = pl.multiple_of(place // 4 * 48, 16)
+            left = pl.multiple_of(place % 4 * 384, 128)
+            was = old[o, pl.ds(top, 48), pl.ds(left, 384)]
+            with_old = lanes_sum(jnp.sum(grad * was, axis=0, keepdims=True))
+            old_old = lanes_sum(jnp.sum(was * was, axis=0, keepdims=True))
+            rest = grad - three(coef_of(with_old, old_old)) * was
+            strecv[o, chan] = packed(
+                with_old, old_old, lanes_sum(jnp.sum(rest * rest, axis=0, keepdims=True))
+            )
+            return share(
+                strecv.at[o, chan],
+                t_send,
+                t_recv,
+                [(d, {"chan": (chan + d) % 4}) for d in range(1, 4)],
+            )
+
         gather = []
         for part in range(PARTS):
             rows, lanes = part_of(part)
@@ -413,41 +441,22 @@
             for i in range(1, depth):
                 total = total + zbuf[o, i, rows, lanes].astype(F32)
             agbuf[o, place, rows, lanes] = total.astype(BF16)
+            if part == PARTS - 1:
+                over_chan = sums_over_chan()
             slot = lambda d: agbuf.at[o, place]
             gather.append(spread_rows(part, plane, slot, slot, a_send, a_recv))
-        grad = agbuf[o, place].astype(F32)
-        top = pl.multiple_of(place // 4 * 48, 16)
-        left = pl.multiple_of(place % 4 * 384, 128)
-        was = old[o, pl.ds(top, 48), pl.ds(left, 384)]
-        with_old = lanes_sum(jnp.sum(grad * was, axis=0, keepdims=True))
-        old_old = lanes_sum(jnp.sum(was * was, axis=0, keepdims=True))
-        part = grad - three(coef_of(with_old, old_old)) * was
-        strecv[o, chan] = packed(
-            with_old, old_old, lanes_sum(jnp.sum(part * part, axis=0, keepdims=True))
-        )
-
-        def share(slot, send, recv, peers):
-            copies = [
-                remote(slot, slot, send.at[o, d], recv.at[o, d], peer) for d, peer in peers
-            ]
-            for copy in copies:
-                copy.start()
-            for copy in copies:
-                copy.wait_recv()
-            sent.extend(copies)
-
-        share(
-            strecv.at[o, chan],
-            t_send,
-            t_recv,
-            [(d, {"chan": (chan + d) % 4}) for d in range(1, 4)],
-        )
+        for copy in over_chan:
+            copy.wait_recv()
         parts = [strecv[o, i] for i in range(4)]
         with_old, old_old = total_of(parts, 0), total_of(parts, 1)
         plane_sums[o, place] = packed(
             with_old, old_old, pooled(parts, coef_of(with_old, old_old))
         )
-        share(plane_sums.at[o, place], u_send, u_recv, [(d, {"tm": peer}) for d, peer in plane])
+        over_plane = share(
+            plane_sums.at[o, place], u_send, u_recv, [(d, {"tm": peer}) for d, peer in plane]
+        )
+        for copy in over_plane:
+            copy.wait_recv()
         parts = [plane_sums[o, i] for i in range(PLANE)]
         mean_sq = total_of(parts, 1)[0:1] / ENTRIES + tiny_eps
         along = total_of(parts, 0)[0:1] / ENTRIES / mean_sq

time: 127 us -> 121 us (0.953)
  Pallas kernels: 117 us -> 111 us
    pallas_call x1, Pallas kernels: 117 us -> 111 us  [shards(): pl.pallas_call(functools.partial(kernel, segments), out_shape=(jax.ShapeD...]
where the time goes in v7:
time: 121 us
  Pallas kernels  111 us (92%)
  local copies, waits for them, and re-layouts  4.89 us (4%)
  other arithmetic  4.67 us (4%)
    pallas_call x1, Pallas kernels, shards(): pl.pallas_call(functools.partial(kernel, segments), out_shape=(jax.ShapeD...  111 us
    unnamed x6, local copies, waits for them, and re-layouts  4.23 us
    select_n x1, other arithmetic, shards(): jnp.where(owner == 1, first, jnp.where(owner == 2, last, dictionary_init))  2.97 us

profile of v7, /device:TPU:1, one launch (start us, length us, event | category | flops | bytes accessed | tf_op | source)
XLA Modules:
  0.0 121.1 jit_solution(8229355903850043446)
XLA Ops:
  0.6 0.7 broadcast_in_dim.23
  1.3 0.7 convert_element_type.3
  2.0 0.8 pad_maximum_fusion.small_ref
  2.9 0.0 copy-start
  2.9 2.3 %copy-done = f32[128,9216]{1,0:T(8,128)S(1)} copy-done((f32[128,9216]{1,0:T(8,128)S(1)}, f32[128,9216]{1,0:T(8,128)}, u32[]{:S(2)}) %copy-start) | copy-done | bytes 4718616
  5.2 0.0 copy-start.1
  5.2 0.7 copy-done.1
  5.9 110.8 %shard_map.76 = (f32[128,128]{1,0:T(8,128)S(1)}, f32[96,128]{1,0:T(8,128)S(1)}, f32[16,9216]{1,0:T(8,128)S(1)}, f32[16,9216]{1,0:T(8,128)S(1)}, s32[128,128]{1,0:T(8,128)S(1)}) custom-call(s32[8]{0:T(128)S(1)} %copy-done.1, f32[128,9216]{1,0:T(8,128)S(1)} %copy-done, f32[232,128]{1,0:T(8,128)S(1)} %pad_maximum_fusion.small_ref), custom_call_target="tpu_custom_call" | custom-call | tf_op jit(solution)/shard_map/pallas_call | solution.py:602
  116.7 0.1 compare_reduce_fusion.1
  116.8 3.0 %fusion = f32[128,9216]{1,0:T(8,128)} fusion(f32[128,9216]{1,0:T(8,128)S(1)} %copy-done, f32[16,9216]{1,0:T(8,128)S(1)} %get-tuple-element.11, f32[16,9216]{1,0:T(8,128)S(1)} %get-tuple-element.10, pred[128]{0:T(512)(128)(4,1)S(1)} %get-tuple-element.14, pred[128]{0:T(512)(128)(4,1)S(1)} %get-tuple-element.13), kind=kLoop, calls=%fused_computation.1 | loop fusion | flops 2359296 | bytes 10617088 | tf_op jit(solution)/shard_map/jit(_where)/select_n | solution.py:667
  119.8 0.6 copy.10
  120.4 0.6 copy.11
Async XLA Ops:
  2.9 2.3 %copy-start = (f32[128,9216]{1,0:T(8,128)S(1)}, f32[128,9216]{1,0:T(8,128)}, u32[]{:S(2)}) copy-start(f32[128,9216]{1,0:T(8,128)} %dict_ref.1) | copy-start | bytes 14155780
  5.2 0.7 copy-start.1
